TPU v7x, 32 devices: a whole 2x2x4 slice. The times are simulated.
32 devices in a mesh: pairs: 2 (over x), band: 16 (over z, y, core).
Axes of the slice: x: 2, y: 2, z: 4, core: 2. Of those that a mesh axis runs over, the one named last changes fastest.
Arguments:
- query_tiles: bfloat16 [512, 256, 128], P(('pairs', 'band')), parts along dimension 0, may hold values from -52 to 52
- target: bfloat16 [512, 256, 128], P(('pairs', 'band')), parts along dimension 0, may hold values from -6 to 6
- tile_home: int32 [512], P('pairs'), parts along dimension 0, may hold values from 0 to 255, as said below
- candidates: int32 [512, 64], P(('pairs', 'band')), parts along dimension 0, may hold values from 0 to 255, as said below
- valid_mask: int32 [512, 64], P(('pairs', 'band')), parts along dimension 0, may hold values from 0 to 1, as said below
Outputs:
- matched: bfloat16 [512, 256, 128], P(('pairs', 'band')), parts along dimension 0
There are 2 independent parts, one for each index of `pairs`. A program takes and returns all parts, laid end to end along the dimension named above; each array names one. Nothing has to cross between parts.
Inputs may be any that keep to these rules, and one draw needn't show every extreme that they name: `tile_home`: a permutation of 0 to 255; target tile ids that agree modulo 16 are stored on the same device, storage row r lying on device r // 16. Ids in a row are distinct; the candidates of one device's query tiles all lie in one run of 128 consecutive ids taken modulo 256, and its first two query tiles together name every id of that run. `valid_mask`: the first entry of every row is 1.
All inputs are finite; a program needn't handle non-finite values.
Results may differ from a plain program's by a relative error of at most 0.0034.
Values may be sent and summed in bfloat16 or wider, within the bound.
No kernel may reach another device: no remote copies, remote signals or barrier semaphores. Data moves between devices by JAX's collectives and lax.ppermute only.
A program may use at most 128 MiB of HBM per device.

v0:
```python
import math
import jax
import jax.numpy as jnp
from jax import lax
from jax.sharding import PartitionSpec as P


def attend_tile(tile_query, tile_keys, keep_mask):
    per_tile = tile_keys.shape[0] // keep_mask.shape[0]
    scores = jnp.dot(tile_query, tile_keys.T, preferred_element_type=jnp.float32) * (
        1.0 / math.sqrt(tile_query.shape[1])
    )
    allowed = jnp.repeat(keep_mask > 0, per_tile)[None, :]
    scores = jnp.where(allowed, scores, -jnp.inf)
    peak = jnp.max(scores, axis=1, keepdims=True)
    raised = jnp.exp(scores - peak)
    totals = jnp.sum(raised, axis=1, keepdims=True)
    weights = (raised / totals).astype(jnp.bfloat16)
    return jnp.dot(weights, tile_keys, preferred_element_type=jnp.float32).astype(jnp.bfloat16)


def body(query_tiles, target, tile_home, candidates, valid_mask):
    channels = target.shape[2]
    stored_rows = tile_home[candidates]
    source = lax.all_gather(target, "band", axis=0, tiled=True)

    def one_tile(packed):
        tile_query, chosen, keep_mask = packed
        stored = source[chosen].reshape(-1, channels)
        return attend_tile(tile_query, stored, keep_mask)

    return lax.map(one_tile, (query_tiles, stored_rows, valid_mask))


def solution(mesh):
    in_specs = (
        P(("pairs", "band"), None, None),
        P(("pairs", "band"), None, None),
        P("pairs"),
        P(("pairs", "band"), None),
        P(("pairs", "band"), None),
    )
    out_specs = P(("pairs", "band"), None, None)
    return jax.shard_map(body, mesh=mesh, in_specs=in_specs, out_specs=out_specs, check_vma=False)
```

profile of v0, /device:TPU:0, one launch (start us, length us, event | category | flops | bytes accessed | tf_op | source)
XLA Modules:
  0.0 721.8 jit_solution(7972578319023650568)
XLA Ops:
  15.0 123.7 %all-gather.2.cloned.1.call-done = bf16[256,256,128]{2,1,0:T(8,128)(2,1)} async-done(((bf16[16,256,128]{2,1,0:T(8,128)(2,1)}), bf16[256,256,128]{2,1,0:T(8,128)(2,1)}) %all-gather.2.cloned.1.call-update) | async-done | bytes 16777232 | tf_op jit(solution)/shard_map/all_gather | solution.py:25
  138.7 575.3 %while.10 = (s32[]{:T(128)}, bf16[16,256,128]{2,1,0:T(8,128)(2,1)S(1)}, s32[16,64]{1,0:T(8,128)}, bf16[16,256,128]{2,1,0:T(8,128)(2,1)}, s32[16,64]{1,0:T(8,128)S(1)}, /*index=5*/bf16[256,256,128]{2,1,0:T(8,128)(2,1)}, s32[]{:T(128)}) while((s32[]{:T(128)}, bf16[16,256,128]{2,1,0:T(8,128)(2,1)S(1)}, s32[16,64]{1,0:T(8,128)}, ...), condition=%wide.region_3.4_spmd, body=%wide.region_0.3_spmd.sunk | while | flops 2181071616 | bytes 84093936 | solution.py:32
  138.7 8.9 %gather_fusion = bf16[64,256,128]{2,1,0:T(8,128)(2,1)} fusion(bf16[256,256,128]{2,1,0:T(8,128)(2,1)} %get-tuple-element.112, s32[1024]{0:T(1024)S(1)} %pad_clamp_fusion.2), kind=kCustom, calls=%fused_computation.clone.1 | custom fusion | bytes 8388864 | tf_op jit(solution)/shard_map/while/body/eval_jaxpr/gather | solution.py:29
  148.4 10.4 %fusion.23 = (f32[256]{0:T(256)S(1)}, f32[256,16384]{1,0:T(8,128)}) fusion(bf16[16384,128]{1,0:T(8,128)(2,1)} %bitcast.38, bf16[16,256,128]{2,1,0:T(8,128)(2,1)} %get-tuple-element.110, s32[]{:T(128)} %get-tuple-element.100, pred[16384]{0:T(1024)(128)(4,1)S(1)} %broadcast_in_dim.37), kind=kOutput, calls=%fused_computation.23.clone.1 | convolution fusion | flops 1086324480 | bytes 21054976 | tf_op jit(solution)/shard_map/while/body/eval_jaxpr/dot_general | solution.py:10
  158.9 8.1 %fusion.24 = f32[256]{0:T(256)S(1)} fusion(f32[256,16384]{1,0:T(8,128)} %get-tuple-element.91, f32[256]{0:T(256)S(1)} %get-tuple-element.92), kind=kLoop, calls=%fused_computation.6.clone.1 | loop fusion | flops 8388352 | bytes 16779264 | tf_op jit(solution)/shard_map/while/body/eval_jaxpr/reduce_sum | solution.py:17
  167.0 7.6 %fusion.25 = bf16[16,256,128]{2,1,0:T(8,128)(2,1)S(1)} fusion(bf16[16,256,128]{2,1,0:T(8,128)(2,1)S(1)} %get-tuple-element.101, s32[]{:T(128)} %get-tuple-element.100, bf16[16384,128]{1,0:T(8,128)(2,1)S(1)} %bitcast.39, f32[256,16384]{1,0:T(8,128)} %get-tuple-element.91, f32[256]{0:T(256)S(1)} %fusion.24, f32[256]{0:T(256)S(1)} %get-tuple-element.92), kind=kOutput, calls=%fused_computation.10.clone.1 | convolution fusion | flops 1086357504 | bytes 21039108 | tf_op jit(solution)/shard_map/while/body/eval_jaxpr/dot_general | solution.py:19
  174.7 8.9 %gather_fusion = bf16[64,256,128]{2,1,0:T(8,128)(2,1)} fusion(bf16[256,256,128]{2,1,0:T(8,128)(2,1)} %get-tuple-element.112, s32[1024]{0:T(1024)S(1)} %pad_clamp_fusion.2), kind=kCustom, calls=%fused_computation.clone.1 | custom fusion | bytes 8388864 | tf_op jit(solution)/shard_map/while/body/eval_jaxpr/gather | solution.py:29
  184.4 10.4 %fusion.23 = (f32[256]{0:T(256)S(1)}, f32[256,16384]{1,0:T(8,128)}) fusion(bf16[16384,128]{1,0:T(8,128)(2,1)} %bitcast.38, bf16[16,256,128]{2,1,0:T(8,128)(2,1)} %get-tuple-element.110, s32[]{:T(128)} %get-tuple-element.100, pred[16384]{0:T(1024)(128)(4,1)S(1)} %broadcast_in_dim.37), kind=kOutput, calls=%fused_computation.23.clone.1 | convolution fusion | flops 1086324480 | bytes 21054976 | tf_op jit(solution)/shard_map/while/body/eval_jaxpr/dot_general | solution.py:10
  194.8 8.1 %fusion.24 = f32[256]{0:T(256)S(1)} fusion(f32[256,16384]{1,0:T(8,128)} %get-tuple-element.91, f32[256]{0:T(256)S(1)} %get-tuple-element.92), kind=kLoop, calls=%fused_computation.6.clone.1 | loop fusion | flops 8388352 | bytes 16779264 | tf_op jit(solution)/shard_map/while/body/eval_jaxpr/reduce_sum | solution.py:17
  203.0 7.6 %fusion.25 = bf16[16,256,128]{2,1,0:T(8,128)(2,1)S(1)} fusion(bf16[16,256,128]{2,1,0:T(8,128)(2,1)S(1)} %get-tuple-element.101, s32[]{:T(128)} %get-tuple-element.100, bf16[16384,128]{1,0:T(8,128)(2,1)S(1)} %bitcast.39, f32[256,16384]{1,0:T(8,128)} %get-tuple-element.91, f32[256]{0:T(256)S(1)} %fusion.24, f32[256]{0:T(256)S(1)} %get-tuple-element.92), kind=kOutput, calls=%fused_computation.10.clone.1 | convolution fusion | flops 1086357504 | bytes 21039108 | tf_op jit(solution)/shard_map/while/body/eval_jaxpr/dot_general | solution.py:19
  210.6 8.9 %gather_fusion = bf16[64,256,128]{2,1,0:T(8,128)(2,1)} fusion(bf16[256,256,128]{2,1,0:T(8,128)(2,1)} %get-tuple-element.112, s32[1024]{0:T(1024)S(1)} %pad_clamp_fusion.2), kind=kCustom, calls=%fused_computation.clone.1 | custom fusion | bytes 8388864 | tf_op jit(solution)/shard_map/while/body/eval_jaxpr/gather | solution.py:29
  220.3 10.4 %fusion.23 = (f32[256]{0:T(256)S(1)}, f32[256,16384]{1,0:T(8,128)}) fusion(bf16[16384,128]{1,0:T(8,128)(2,1)} %bitcast.38, bf16[16,256,128]{2,1,0:T(8,128)(2,1)} %get-tuple-element.110, s32[]{:T(128)} %get-tuple-element.100, pred[16384]{0:T(1024)(128)(4,1)S(1)} %broadcast_in_dim.37), kind=kOutput, calls=%fused_computation.23.clone.1 | convolution fusion | flops 1086324480 | bytes 21054976 | tf_op jit(solution)/shard_map/while/body/eval_jaxpr/dot_general | solution.py:10
  230.8 8.1 %fusion.24 = f32[256]{0:T(256)S(1)} fusion(f32[256,16384]{1,0:T(8,128)} %get-tuple-element.91, f32[256]{0:T(256)S(1)} %get-tuple-element.92), kind=kLoop, calls=%fused_computation.6.clone.1 | loop fusion | flops 8388352 | bytes 16779264 | tf_op jit(solution)/shard_map/while/body/eval_jaxpr/reduce_sum | solution.py:17
  238.9 7.6 %fusion.25 = bf16[16,256,128]{2,1,0:T(8,128)(2,1)S(1)} fusion(bf16[16,256,128]{2,1,0:T(8,128)(2,1)S(1)} %get-tuple-element.101, s32[]{:T(128)} %get-tuple-element.100, bf16[16384,128]{1,0:T(8,128)(2,1)S(1)} %bitcast.39, f32[256,16384]{1,0:T(8,128)} %get-tuple-element.91, f32[256]{0:T(256)S(1)} %fusion.24, f32[256]{0:T(256)S(1)} %get-tuple-element.92), kind=kOutput, calls=%fused_computation.10.clone.1 | convolution fusion | flops 1086357504 | bytes 21039108 | tf_op jit(solution)/shard_map/while/body/eval_jaxpr/dot_general | solution.py:19
  246.6 8.9 %gather_fusion = bf16[64,256,128]{2,1,0:T(8,128)(2,1)} fusion(bf16[256,256,128]{2,1,0:T(8,128)(2,1)} %get-tuple-element.112, s32[1024]{0:T(1024)S(1)} %pad_clamp_fusion.2), kind=kCustom, calls=%fused_computation.clone.1 | custom fusion | bytes 8388864 | tf_op jit(solution)/shard_map/while/body/eval_jaxpr/gather | solution.py:29
  256.3 10.4 %fusion.23 = (f32[256]{0:T(256)S(1)}, f32[256,16384]{1,0:T(8,128)}) fusion(bf16[16384,128]{1,0:T(8,128)(2,1)} %bitcast.38, bf16[16,256,128]{2,1,0:T(8,128)(2,1)} %get-tuple-element.110, s32[]{:T(128)} %get-tuple-element.100, pred[16384]{0:T(1024)(128)(4,1)S(1)} %broadcast_in_dim.37), kind=kOutput, calls=%fused_computation.23.clone.1 | convolution fusion | flops 1086324480 | bytes 21054976 | tf_op jit(solution)/shard_map/while/body/eval_jaxpr/dot_general | solution.py:10
  266.7 8.1 %fusion.24 = f32[256]{0:T(256)S(1)} fusion(f32[256,16384]{1,0:T(8,128)} %get-tuple-element.91, f32[256]{0:T(256)S(1)} %get-tuple-element.92), kind=kLoop, calls=%fused_computation.6.clone.1 | loop fusion | flops 8388352 | bytes 16779264 | tf_op jit(solution)/shard_map/while/body/eval_jaxpr/reduce_sum | solution.py:17
  274.9 7.6 %fusion.25 = bf16[16,256,128]{2,1,0:T(8,128)(2,1)S(1)} fusion(bf16[16,256,128]{2,1,0:T(8,128)(2,1)S(1)} %get-tuple-element.101, s32[]{:T(128)} %get-tuple-element.100, bf16[16384,128]{1,0:T(8,128)(2,1)S(1)} %bitcast.39, f32[256,16384]{1,0:T(8,128)} %get-tuple-element.91, f32[256]{0:T(256)S(1)} %fusion.24, f32[256]{0:T(256)S(1)} %get-tuple-element.92), kind=kOutput, calls=%fused_computation.10.clone.1 | convolution fusion | flops 1086357504 | bytes 21039108 | tf_op jit(solution)/shard_map/while/body/eval_jaxpr/dot_general | solution.py:19
  282.5 8.9 %gather_fusion = bf16[64,256,128]{2,1,0:T(8,128)(2,1)} fusion(bf16[256,256,128]{2,1,0:T(8,128)(2,1)} %get-tuple-element.112, s32[1024]{0:T(1024)S(1)} %pad_clamp_fusion.2), kind=kCustom, calls=%fused_computation.clone.1 | custom fusion | bytes 8388864 | tf_op jit(solution)/shard_map/while/body/eval_jaxpr/gather | solution.py:29
  292.2 10.4 %fusion.23 = (f32[256]{0:T(256)S(1)}, f32[256,16384]{1,0:T(8,128)}) fusion(bf16[16384,128]{1,0:T(8,128)(2,1)} %bitcast.38, bf16[16,256,128]{2,1,0:T(8,128)(2,1)} %get-tuple-element.110, s32[]{:T(128)} %get-tuple-element.100, pred[16384]{0:T(1024)(128)(4,1)S(1)} %broadcast_in_dim.37), kind=kOutput, calls=%fused_computation.23.clone.1 | convolution fusion | flops 1086324480 | bytes 21054976 | tf_op jit(solution)/shard_map/while/body/eval_jaxpr/dot_general | solution.py:10
  302.7 8.1 %fusion.24 = f32[256]{0:T(256)S(1)} fusion(f32[256,16384]{1,0:T(8,128)} %get-tuple-element.91, f32[256]{0:T(256)S(1)} %get-tuple-element.92), kind=kLoop, calls=%fused_computation.6.clone.1 | loop fusion | flops 8388352 | bytes 16779264 | tf_op jit(solution)/shard_map/while/body/eval_jaxpr/reduce_sum | solution.py:17
  310.8 7.6 %fusion.25 = bf16[16,256,128]{2,1,0:T(8,128)(2,1)S(1)} fusion(bf16[16,256,128]{2,1,0:T(8,128)(2,1)S(1)} %get-tuple-element.101, s32[]{:T(128)} %get-tuple-element.100, bf16[16384,128]{1,0:T(8,128)(2,1)S(1)} %bitcast.39, f32[256,16384]{1,0:T(8,128)} %get-tuple-element.91, f32[256]{0:T(256)S(1)} %fusion.24, f32[256]{0:T(256)S(1)} %get-tuple-element.92), kind=kOutput, calls=%fused_computation.10.clone.1 | convolution fusion | flops 1086357504 | bytes 21039108 | tf_op jit(solution)/shard_map/while/body/eval_jaxpr/dot_general | solution.py:19
  318.5 8.9 %gather_fusion = bf16[64,256,128]{2,1,0:T(8,128)(2,1)} fusion(bf16[256,256,128]{2,1,0:T(8,128)(2,1)} %get-tuple-element.112, s32[1024]{0:T(1024)S(1)} %pad_clamp_fusion.2), kind=kCustom, calls=%fused_computation.clone.1 | custom fusion | bytes 8388864 | tf_op jit(solution)/shard_map/while/body/eval_jaxpr/gather | solution.py:29
  328.2 10.4 %fusion.23 = (f32[256]{0:T(256)S(1)}, f32[256,16384]{1,0:T(8,128)}) fusion(bf16[16384,128]{1,0:T(8,128)(2,1)} %bitcast.38, bf16[16,256,128]{2,1,0:T(8,128)(2,1)} %get-tuple-element.110, s32[]{:T(128)} %get-tuple-element.100, pred[16384]{0:T(1024)(128)(4,1)S(1)} %broadcast_in_dim.37), kind=kOutput, calls=%fused_computation.23.clone.1 | convolution fusion | flops 1086324480 | bytes 21054976 | tf_op jit(solution)/shard_map/while/body/eval_jaxpr/dot_general | solution.py:10
  338.6 8.1 %fusion.24 = f32[256]{0:T(256)S(1)} fusion(f32[256,16384]{1,0:T(8,128)} %get-tuple-element.91, f32[256]{0:T(256)S(1)} %get-tuple-element.92), kind=kLoop, calls=%fused_computation.6.clone.1 | loop fusion | flops 8388352 | bytes 16779264 | tf_op jit(solution)/shard_map/while/body/eval_jaxpr/reduce_sum | solution.py:17
  346.8 7.6 %fusion.25 = bf16[16,256,128]{2,1,0:T(8,128)(2,1)S(1)} fusion(bf16[16,256,128]{2,1,0:T(8,128)(2,1)S(1)} %get-tuple-element.101, s32[]{:T(128)} %get-tuple-element.100, bf16[16384,128]{1,0:T(8,128)(2,1)S(1)} %bitcast.39, f32[256,16384]{1,0:T(8,128)} %get-tuple-element.91, f32[256]{0:T(256)S(1)} %fusion.24, f32[256]{0:T(256)S(1)} %get-tuple-element.92), kind=kOutput, calls=%fused_computation.10.clone.1 | convolution fusion | flops 1086357504 | bytes 21039108 | tf_op jit(solution)/shard_map/while/body/eval_jaxpr/dot_general | solution.py:19
  354.5 8.9 %gather_fusion = bf16[64,256,128]{2,1,0:T(8,128)(2,1)} fusion(bf16[256,256,128]{2,1,0:T(8,128)(2,1)} %get-tuple-element.112, s32[1024]{0:T(1024)S(1)} %pad_clamp_fusion.2), kind=kCustom, calls=%fused_computation.clone.1 | custom fusion | bytes 8388864 | tf_op jit(solution)/shard_map/while/body/eval_jaxpr/gather | solution.py:29
  364.2 10.4 %fusion.23 = (f32[256]{0:T(256)S(1)}, f32[256,16384]{1,0:T(8,128)}) fusion(bf16[16384,128]{1,0:T(8,128)(2,1)} %bitcast.38, bf16[16,256,128]{2,1,0:T(8,128)(2,1)} %get-tuple-element.110, s32[]{:T(128)} %get-tuple-element.100, pred[16384]{0:T(1024)(128)(4,1)S(1)} %broadcast_in_dim.37), kind=kOutput, calls=%fused_computation.23.clone.1 | convolution fusion | flops 1086324480 | bytes 21054976 | tf_op jit(solution)/shard_map/while/body/eval_jaxpr/dot_general | solution.py:10
  374.6 8.1 %fusion.24 = f32[256]{0:T(256)S(1)} fusion(f32[256,16384]{1,0:T(8,128)} %get-tuple-element.91, f32[256]{0:T(256)S(1)} %get-tuple-element.92), kind=kLoop, calls=%fused_computation.6.clone.1 | loop fusion | flops 8388352 | bytes 16779264 | tf_op jit(solution)/shard_map/while/body/eval_jaxpr/reduce_sum | solution.py:17
  382.8 7.6 %fusion.25 = bf16[16,256,128]{2,1,0:T(8,128)(2,1)S(1)} fusion(bf16[16,256,128]{2,1,0:T(8,128)(2,1)S(1)} %get-tuple-element.101, s32[]{:T(128)} %get-tuple-element.100, bf16[16384,128]{1,0:T(8,128)(2,1)S(1)} %bitcast.39, f32[256,16384]{1,0:T(8,128)} %get-tuple-element.91, f32[256]{0:T(256)S(1)} %fusion.24, f32[256]{0:T(256)S(1)} %get-tuple-element.92), kind=kOutput, calls=%fused_computation.10.clone.1 | convolution fusion | flops 1086357504 | bytes 21039108 | tf_op jit(solution)/shard_map/while/body/eval_jaxpr/dot_general | solution.py:19
  390.4 8.9 %gather_fusion = bf16[64,256,128]{2,1,0:T(8,128)(2,1)} fusion(bf16[256,256,128]{2,1,0:T(8,128)(2,1)} %get-tuple-element.112, s32[1024]{0:T(1024)S(1)} %pad_clamp_fusion.2), kind=kCustom, calls=%fused_computation.clone.1 | custom fusion | bytes 8388864 | tf_op jit(solution)/shard_map/while/body/eval_jaxpr/gather | solution.py:29
  400.1 10.4 %fusion.23 = (f32[256]{0:T(256)S(1)}, f32[256,16384]{1,0:T(8,128)}) fusion(bf16[16384,128]{1,0:T(8,128)(2,1)} %bitcast.38, bf16[16,256,128]{2,1,0:T(8,128)(2,1)} %get-tuple-element.110, s32[]{:T(128)} %get-tuple-element.100, pred[16384]{0:T(1024)(128)(4,1)S(1)} %broadcast_in_dim.37), kind=kOutput, calls=%fused_computation.23.clone.1 | convolution fusion | flops 1086324480 | bytes 21054976 | tf_op jit(solution)/shard_map/while/body/eval_jaxpr/dot_general | solution.py:10
  410.6 8.1 %fusion.24 = f32[256]{0:T(256)S(1)} fusion(f32[256,16384]{1,0:T(8,128)} %get-tuple-element.91, f32[256]{0:T(256)S(1)} %get-tuple-element.92), kind=kLoop, calls=%fused_computation.6.clone.1 | loop fusion | flops 8388352 | bytes 16779264 | tf_op jit(solution)/shard_map/while/body/eval_jaxpr/reduce_sum | solution.py:17
  418.7 7.6 %fusion.25 = bf16[16,256,128]{2,1,0:T(8,128)(2,1)S(1)} fusion(bf16[16,256,128]{2,1,0:T(8,128)(2,1)S(1)} %get-tuple-element.101, s32[]{:T(128)} %get-tuple-element.100, bf16[16384,128]{1,0:T(8,128)(2,1)S(1)} %bitcast.39, f32[256,16384]{1,0:T(8,128)} %get-tuple-element.91, f32[256]{0:T(256)S(1)} %fusion.24, f32[256]{0:T(256)S(1)} %get-tuple-element.92), kind=kOutput, calls=%fused_computation.10.clone.1 | convolution fusion | flops 1086357504 | bytes 21039108 | tf_op jit(solution)/shard_map/while/body/eval_jaxpr/dot_general | solution.py:19
  426.4 8.9 %gather_fusion = bf16[64,256,128]{2,1,0:T(8,128)(2,1)} fusion(bf16[256,256,128]{2,1,0:T(8,128)(2,1)} %get-tuple-element.112, s32[1024]{0:T(1024)S(1)} %pad_clamp_fusion.2), kind=kCustom, calls=%fused_computation.clone.1 | custom fusion | bytes 8388864 | tf_op jit(solution)/shard_map/while/body/eval_jaxpr/gather | solution.py:29
  436.1 10.4 %fusion.23 = (f32[256]{0:T(256)S(1)}, f32[256,16384]{1,0:T(8,128)}) fusion(bf16[16384,128]{1,0:T(8,128)(2,1)} %bitcast.38, bf16[16,256,128]{2,1,0:T(8,128)(2,1)} %get-tuple-element.110, s32[]{:T(128)} %get-tuple-element.100, pred[16384]{0:T(1024)(128)(4,1)S(1)} %broadcast_in_dim.37), kind=kOutput, calls=%fused_computation.23.clone.1 | convolution fusion | flops 1086324480 | bytes 21054976 | tf_op jit(solution)/shard_map/while/body/eval_jaxpr/dot_general | solution.py:10
  446.5 8.1 %fusion.24 = f32[256]{0:T(256)S(1)} fusion(f32[256,16384]{1,0:T(8,128)} %get-tuple-element.91, f32[256]{0:T(256)S(1)} %get-tuple-element.92), kind=kLoop, calls=%fused_computation.6.clone.1 | loop fusion | flops 8388352 | bytes 16779264 | tf_op jit(solution)/shard_map/while/body/eval_jaxpr/reduce_sum | solution.py:17
  454.7 7.6 %fusion.25 = bf16[16,256,128]{2,1,0:T(8,128)(2,1)S(1)} fusion(bf16[16,256,128]{2,1,0:T(8,128)(2,1)S(1)} %get-tuple-element.101, s32[]{:T(128)} %get-tuple-element.100, bf16[16384,128]{1,0:T(8,128)(2,1)S(1)} %bitcast.39, f32[256,16384]{1,0:T(8,128)} %get-tuple-element.91, f32[256]{0:T(256)S(1)} %fusion.24, f32[256]{0:T(256)S(1)} %get-tuple-element.92), kind=kOutput, calls=%fused_computation.10.clone.1 | convolution fusion | flops 1086357504 | bytes 21039108 | tf_op jit(solution)/shard_map/while/body/eval_jaxpr/dot_general | solution.py:19
  462.3 8.9 %gather_fusion = bf16[64,256,128]{2,1,0:T(8,128)(2,1)} fusion(bf16[256,256,128]{2,1,0:T(8,128)(2,1)} %get-tuple-element.112, s32[1024]{0:T(1024)S(1)} %pad_clamp_fusion.2), kind=kCustom, calls=%fused_computation.clone.1 | custom fusion | bytes 8388864 | tf_op jit(solution)/shard_map/while/body/eval_jaxpr/gather | solution.py:29
  472.0 10.4 %fusion.23 = (f32[256]{0:T(256)S(1)}, f32[256,16384]{1,0:T(8,128)}) fusion(bf16[16384,128]{1,0:T(8,128)(2,1)} %bitcast.38, bf16[16,256,128]{2,1,0:T(8,128)(2,1)} %get-tuple-element.110, s32[]{:T(128)} %get-tuple-element.100, pred[16384]{0:T(1024)(128)(4,1)S(1)} %broadcast_in_dim.37), kind=kOutput, calls=%fused_computation.23.clone.1 | convolution fusion | flops 1086324480 | bytes 21054976 | tf_op jit(solution)/shard_map/while/body/eval_jaxpr/dot_general | solution.py:10
  482.5 8.1 %fusion.24 = f32[256]{0:T(256)S(1)} fusion(f32[256,16384]{1,0:T(8,128)} %get-tuple-element.91, f32[256]{0:T(256)S(1)} %get-tuple-element.92), kind=kLoop, calls=%fused_computation.6.clone.1 | loop fusion | flops 8388352 | bytes 16779264 | tf_op jit(solution)/shard_map/while/body/eval_jaxpr/reduce_sum | solution.py:17
  490.6 7.6 %fusion.25 = bf16[16,256,128]{2,1,0:T(8,128)(2,1)S(1)} fusion(bf16[16,256,128]{2,1,0:T(8,128)(2,1)S(1)} %get-tuple-element.101, s32[]{:T(128)} %get-tuple-element.100, bf16[16384,128]{1,0:T(8,128)(2,1)S(1)} %bitcast.39, f32[256,16384]{1,0:T(8,128)} %get-tuple-element.91, f32[256]{0:T(256)S(1)} %fusion.24, f32[256]{0:T(256)S(1)} %get-tuple-element.92), kind=kOutput, calls=%fused_computation.10.clone.1 | convolution fusion | flops 1086357504 | bytes 21039108 | tf_op jit(solution)/shard_map/while/body/eval_jaxpr/dot_general | solution.py:19
  498.3 8.9 %gather_fusion = bf16[64,256,128]{2,1,0:T(8,128)(2,1)} fusion(bf16[256,256,128]{2,1,0:T(8,128)(2,1)} %get-tuple-element.112, s32[1024]{0:T(1024)S(1)} %pad_clamp_fusion.2), kind=kCustom, calls=%fused_computation.clone.1 | custom fusion | bytes 8388864 | tf_op jit(solution)/shard_map/while/body/eval_jaxpr/gather | solution.py:29
  508.0 10.4 %fusion.23 = (f32[256]{0:T(256)S(1)}, f32[256,16384]{1,0:T(8,128)}) fusion(bf16[16384,128]{1,0:T(8,128)(2,1)} %bitcast.38, bf16[16,256,128]{2,1,0:T(8,128)(2,1)} %get-tuple-element.110, s32[]{:T(128)} %get-tuple-element.100, pred[16384]{0:T(1024)(128)(4,1)S(1)} %broadcast_in_dim.37), kind=kOutput, calls=%fused_computation.23.clone.1 | convolution fusion | flops 1086324480 | bytes 21054976 | tf_op jit(solution)/shard_map/while/body/eval_jaxpr/dot_general | solution.py:10
  518.4 8.1 %fusion.24 = f32[256]{0:T(256)S(1)} fusion(f32[256,16384]{1,0:T(8,128)} %get-tuple-element.91, f32[256]{0:T(256)S(1)} %get-tuple-element.92), kind=kLoop, calls=%fused_computation.6.clone.1 | loop fusion | flops 8388352 | bytes 16779264 | tf_op jit(solution)/shard_map/while/body/eval_jaxpr/reduce_sum | solution.py:17
  526.6 7.6 %fusion.25 = bf16[16,256,128]{2,1,0:T(8,128)(2,1)S(1)} fusion(bf16[16,256,128]{2,1,0:T(8,128)(2,1)S(1)} %get-tuple-element.101, s32[]{:T(128)} %get-tuple-element.100, bf16[16384,128]{1,0:T(8,128)(2,1)S(1)} %bitcast.39, f32[256,16384]{1,0:T(8,128)} %get-tuple-element.91, f32[256]{0:T(256)S(1)} %fusion.24, f32[256]{0:T(256)S(1)} %get-tuple-element.92), kind=kOutput, calls=%fused_computation.10.clone.1 | convolution fusion | flops 1086357504 | bytes 21039108 | tf_op jit(solution)/shard_map/while/body/eval_jaxpr/dot_general | solution.py:19
  534.2 8.9 %gather_fusion = bf16[64,256,128]{2,1,0:T(8,128)(2,1)} fusion(bf16[256,256,128]{2,1,0:T(8,128)(2,1)} %get-tuple-element.112, s32[1024]{0:T(1024)S(1)} %pad_clamp_fusion.2), kind=kCustom, calls=%fused_computation.clone.1 | custom fusion | bytes 8388864 | tf_op jit(solution)/shard_map/while/body/eval_jaxpr/gather | solution.py:29
  544.0 10.4 %fusion.23 = (f32[256]{0:T(256)S(1)}, f32[256,16384]{1,0:T(8,128)}) fusion(bf16[16384,128]{1,0:T(8,128)(2,1)} %bitcast.38, bf16[16,256,128]{2,1,0:T(8,128)(2,1)} %get-tuple-element.110, s32[]{:T(128)} %get-tuple-element.100, pred[16384]{0:T(1024)(128)(4,1)S(1)} %broadcast_in_dim.37), kind=kOutput, calls=%fused_computation.23.clone.1 | convolution fusion | flops 1086324480 | bytes 21054976 | tf_op jit(solution)/shard_map/while/body/eval_jaxpr/dot_general | solution.py:10
  554.4 8.1 %fusion.24 = f32[256]{0:T(256)S(1)} fusion(f32[256,16384]{1,0:T(8,128)} %get-tuple-element.91, f32[256]{0:T(256)S(1)} %get-tuple-element.92), kind=kLoop, calls=%fused_computation.6.clone.1 | loop fusion | flops 8388352 | bytes 16779264 | tf_op jit(solution)/shard_map/while/body/eval_jaxpr/reduce_sum | solution.py:17
  562.5 7.6 %fusion.25 = bf16[16,256,128]{2,1,0:T(8,128)(2,1)S(1)} fusion(bf16[16,256,128]{2,1,0:T(8,128)(2,1)S(1)} %get-tuple-element.101, s32[]{:T(128)} %get-tuple-element.100, bf16[16384,128]{1,0:T(8,128)(2,1)S(1)} %bitcast.39, f32[256,16384]{1,0:T(8,128)} %get-tuple-element.91, f32[256]{0:T(256)S(1)} %fusion.24, f32[256]{0:T(256)S(1)} %get-tuple-element.92), kind=kOutput, calls=%fused_computation.10.clone.1 | convolution fusion | flops 1086357504 | bytes 21039108 | tf_op jit(solution)/shard_map/while/body/eval_jaxpr/dot_general | solution.py:19
  570.2 8.9 %gather_fusion = bf16[64,256,128]{2,1,0:T(8,128)(2,1)} fusion(bf16[256,256,128]{2,1,0:T(8,128)(2,1)} %get-tuple-element.112, s32[1024]{0:T(1024)S(1)} %pad_clamp_fusion.2), kind=kCustom, calls=%fused_computation.clone.1 | custom fusion | bytes 8388864 | tf_op jit(solution)/shard_map/while/body/eval_jaxpr/gather | solution.py:29
  579.9 10.4 %fusion.23 = (f32[256]{0:T(256)S(1)}, f32[256,16384]{1,0:T(8,128)}) fusion(bf16[16384,128]{1,0:T(8,128)(2,1)} %bitcast.38, bf16[16,256,128]{2,1,0:T(8,128)(2,1)} %get-tuple-element.110, s32[]{:T(128)} %get-tuple-element.100, pred[16384]{0:T(1024)(128)(4,1)S(1)} %broadcast_in_dim.37), kind=kOutput, calls=%fused_computation.23.clone.1 | convolution fusion | flops 1086324480 | bytes 21054976 | tf_op jit(solution)/shard_map/while/body/eval_jaxpr/dot_general | solution.py:10
  590.4 8.1 %fusion.24 = f32[256]{0:T(256)S(1)} fusion(f32[256,16384]{1,0:T(8,128)} %get-tuple-element.91, f32[256]{0:T(256)S(1)} %get-tuple-element.92), kind=kLoop, calls=%fused_computation.6.clone.1 | loop fusion | flops 8388352 | bytes 16779264 | tf_op jit(solution)/shard_map/while/body/eval_jaxpr/reduce_sum | solution.py:17
  598.5 7.6 %fusion.25 = bf16[16,256,128]{2,1,0:T(8,128)(2,1)S(1)} fusion(bf16[16,256,128]{2,1,0:T(8,128)(2,1)S(1)} %get-tuple-element.101, s32[]{:T(128)} %get-tuple-element.100, bf16[16384,128]{1,0:T(8,128)(2,1)S(1)} %bitcast.39, f32[256,16384]{1,0:T(8,128)} %get-tuple-element.91, f32[256]{0:T(256)S(1)} %fusion.24, f32[256]{0:T(256)S(1)} %get-tuple-element.92), kind=kOutput, calls=%fused_computation.10.clone.1 | convolution fusion | flops 1086357504 | bytes 21039108 | tf_op jit(solution)/shard_map/while/body/eval_jaxpr/dot_general | solution.py:19
  606.2 8.9 %gather_fusion = bf16[64,256,128]{2,1,0:T(8,128)(2,1)} fusion(bf16[256,256,128]{2,1,0:T(8,128)(2,1)} %get-tuple-element.112, s32[1024]{0:T(1024)S(1)} %pad_clamp_fusion.2), kind=kCustom, calls=%fused_computation.clone.1 | custom fusion | bytes 8388864 | tf_op jit(solution)/shard_map/while/body/eval_jaxpr/gather | solution.py:29
  615.9 10.4 %fusion.23 = (f32[256]{0:T(256)S(1)}, f32[256,16384]{1,0:T(8,128)}) fusion(bf16[16384,128]{1,0:T(8,128)(2,1)} %bitcast.38, bf16[16,256,128]{2,1,0:T(8,128)(2,1)} %get-tuple-element.110, s32[]{:T(128)} %get-tuple-element.100, pred[16384]{0:T(1024)(128)(4,1)S(1)} %broadcast_in_dim.37), kind=kOutput, calls=%fused_computation.23.clone.1 | convolution fusion | flops 1086324480 | bytes 21054976 | tf_op jit(solution)/shard_map/while/body/eval_jaxpr/dot_general | solution.py:10
  626.3 8.1 %fusion.24 = f32[256]{0:T(256)S(1)} fusion(f32[256,16384]{1,0:T(8,128)} %get-tuple-element.91, f32[256]{0:T(256)S(1)} %get-tuple-element.92), kind=kLoop, calls=%fused_computation.6.clone.1 | loop fusion | flops 8388352 | bytes 16779264 | tf_op jit(solution)/shard_map/while/body/eval_jaxpr/reduce_sum | solution.py:17
  642.1 8.9 %gather_fusion = bf16[64,256,128]{2,1,0:T(8,128)(2,1)} fusion(bf16[256,256,128]{2,1,0:T(8,128)(2,1)} %get-tuple-element.112, s32[1024]{0:T(1024)S(1)} %pad_clamp_fusion.2), kind=kCustom, calls=%fused_computation.clone.1 | custom fusion | bytes 8388864 | tf_op jit(solution)/shard_map/while/body/eval_jaxpr/gather | solution.py:29
  651.8 10.4 %fusion.23 = (f32[256]{0:T(256)S(1)}, f32[256,16384]{1,0:T(8,128)}) fusion(bf16[16384,128]{1,0:T(8,128)(2,1)} %bitcast.38, bf16[16,256,128]{2,1,0:T(8,128)(2,1)} %get-tuple-element.110, s32[]{:T(128)} %get-tuple-element.100, pred[16384]{0:T(1024)(128)(4,1)S(1)} %broadcast_in_dim.37), kind=kOutput, calls=%fused_computation.23.clone.1 | convolution fusion | flops 1086324480 | bytes 21054976 | tf_op jit(solution)/shard_map/while/body/eval_jaxpr/dot_general | solution.py:10
  662.3 8.1 %fusion.24 = f32[256]{0:T(256)S(1)} fusion(f32[256,16384]{1,0:T(8,128)} %get-tuple-element.91, f32[256]{0:T(256)S(1)} %get-tuple-element.92), kind=kLoop, calls=%fused_computation.6.clone.1 | loop fusion | flops 8388352 | bytes 16779264 | tf_op jit(solution)/shard_map/while/body/eval_jaxpr/reduce_sum | solution.py:17
  678.1 8.9 %gather_fusion = bf16[64,256,128]{2,1,0:T(8,128)(2,1)} fusion(bf16[256,256,128]{2,1,0:T(8,128)(2,1)} %get-tuple-element.112, s32[1024]{0:T(1024)S(1)} %pad_clamp_fusion.2), kind=kCustom, calls=%fused_computation.clone.1 | custom fusion | bytes 8388864 | tf_op jit(solution)/shard_map/while/body/eval_jaxpr/gather | solution.py:29
  687.8 10.4 %fusion.23 = (f32[256]{0:T(256)S(1)}, f32[256,16384]{1,0:T(8,128)}) fusion(bf16[16384,128]{1,0:T(8,128)(2,1)} %bitcast.38, bf16[16,256,128]{2,1,0:T(8,128)(2,1)} %get-tuple-element.110, s32[]{:T(128)} %get-tuple-element.100, pred[16384]{0:T(1024)(128)(4,1)S(1)} %broadcast_in_dim.37), kind=kOutput, calls=%fused_computation.23.clone.1 | convolution fusion | flops 1086324480 | bytes 21054976 | tf_op jit(solution)/shard_map/while/body/eval_jaxpr/dot_general | solution.py:10
  698.2 8.1 %fusion.24 = f32[256]{0:T(256)S(1)} fusion(f32[256,16384]{1,0:T(8,128)} %get-tuple-element.91, f32[256]{0:T(256)S(1)} %get-tuple-element.92), kind=kLoop, calls=%fused_computation.6.clone.1 | loop fusion | flops 8388352 | bytes 16779264 | tf_op jit(solution)/shard_map/while/body/eval_jaxpr/reduce_sum | solution.py:17
  706.4 7.6 %fusion.25 = bf16[16,256,128]{2,1,0:T(8,128)(2,1)S(1)} fusion(bf16[16,256,128]{2,1,0:T(8,128)(2,1)S(1)} %get-tuple-element.101, s32[]{:T(128)} %get-tuple-element.100, bf16[16384,128]{1,0:T(8,128)(2,1)S(1)} %bitcast.39, f32[256,16384]{1,0:T(8,128)} %get-tuple-element.91, f32[256]{0:T(256)S(1)} %fusion.24, f32[256]{0:T(256)S(1)} %get-tuple-element.92), kind=kOutput, calls=%fused_computation.10.clone.1 | convolution fusion | flops 1086357504 | bytes 21039108 | tf_op jit(solution)/shard_map/while/body/eval_jaxpr/dot_general | solution.py:19
  (126 shorter events, 37.6 us)
Async XLA Ops:
  6.5 1.5 copy-start
  6.5 132.1 %all-gather.2.cloned.1.call-start = ((), (), s32[]{:S(2)}) async-start(), calls=%async_computation | async-start | bytes 17825792 | tf_op jit(solution)/shard_map/all_gather | solution.py:25
  148.4 18.6 %copy-start.1 = (bf16[64,256,128]{2,1,0:T(8,128)(2,1)S(1)}, bf16[64,256,128]{2,1,0:T(8,128)(2,1)}, u32[]{:S(2)}) copy-start(bf16[64,256,128]{2,1,0:T(8,128)(2,1)} %gather_fusion) | copy-start | bytes 12582916 | tf_op jit(solution)/shard_map/while
  184.4 18.6 %copy-start.1 = (bf16[64,256,128]{2,1,0:T(8,128)(2,1)S(1)}, bf16[64,256,128]{2,1,0:T(8,128)(2,1)}, u32[]{:S(2)}) copy-start(bf16[64,256,128]{2,1,0:T(8,128)(2,1)} %gather_fusion) | copy-start | bytes 12582916 | tf_op jit(solution)/shard_map/while
  220.3 18.6 %copy-start.1 = (bf16[64,256,128]{2,1,0:T(8,128)(2,1)S(1)}, bf16[64,256,128]{2,1,0:T(8,128)(2,1)}, u32[]{:S(2)}) copy-start(bf16[64,256,128]{2,1,0:T(8,128)(2,1)} %gather_fusion) | copy-start | bytes 12582916 | tf_op jit(solution)/shard_map/while
  256.3 18.6 %copy-start.1 = (bf16[64,256,128]{2,1,0:T(8,128)(2,1)S(1)}, bf16[64,256,128]{2,1,0:T(8,128)(2,1)}, u32[]{:S(2)}) copy-start(bf16[64,256,128]{2,1,0:T(8,128)(2,1)} %gather_fusion) | copy-start | bytes 12582916 | tf_op jit(solution)/shard_map/while
  292.2 18.6 %copy-start.1 = (bf16[64,256,128]{2,1,0:T(8,128)(2,1)S(1)}, bf16[64,256,128]{2,1,0:T(8,128)(2,1)}, u32[]{:S(2)}) copy-start(bf16[64,256,128]{2,1,0:T(8,128)(2,1)} %gather_fusion) | copy-start | bytes 12582916 | tf_op jit(solution)/shard_map/while
  328.2 18.6 %copy-start.1 = (bf16[64,256,128]{2,1,0:T(8,128)(2,1)S(1)}, bf16[64,256,128]{2,1,0:T(8,128)(2,1)}, u32[]{:S(2)}) copy-start(bf16[64,256,128]{2,1,0:T(8,128)(2,1)} %gather_fusion) | copy-start | bytes 12582916 | tf_op jit(solution)/shard_map/while
  364.2 18.6 %copy-start.1 = (bf16[64,256,128]{2,1,0:T(8,128)(2,1)S(1)}, bf16[64,256,128]{2,1,0:T(8,128)(2,1)}, u32[]{:S(2)}) copy-start(bf16[64,256,128]{2,1,0:T(8,128)(2,1)} %gather_fusion) | copy-start | bytes 12582916 | tf_op jit(solution)/shard_map/while
  400.1 18.6 %copy-start.1 = (bf16[64,256,128]{2,1,0:T(8,128)(2,1)S(1)}, bf16[64,256,128]{2,1,0:T(8,128)(2,1)}, u32[]{:S(2)}) copy-start(bf16[64,256,128]{2,1,0:T(8,128)(2,1)} %gather_fusion) | copy-start | bytes 12582916 | tf_op jit(solution)/shard_map/while
  436.1 18.6 %copy-start.1 = (bf16[64,256,128]{2,1,0:T(8,128)(2,1)S(1)}, bf16[64,256,128]{2,1,0:T(8,128)(2,1)}, u32[]{:S(2)}) copy-start(bf16[64,256,128]{2,1,0:T(8,128)(2,1)} %gather_fusion) | copy-start | bytes 12582916 | tf_op jit(solution)/shard_map/while
  472.0 18.6 %copy-start.1 = (bf16[64,256,128]{2,1,0:T(8,128)(2,1)S(1)}, bf16[64,256,128]{2,1,0:T(8,128)(2,1)}, u32[]{:S(2)}) copy-start(bf16[64,256,128]{2,1,0:T(8,128)(2,1)} %gather_fusion) | copy-start | bytes 12582916 | tf_op jit(solution)/shard_map/while
  508.0 18.6 %copy-start.1 = (bf16[64,256,128]{2,1,0:T(8,128)(2,1)S(1)}, bf16[64,256,128]{2,1,0:T(8,128)(2,1)}, u32[]{:S(2)}) copy-start(bf16[64,256,128]{2,1,0:T(8,128)(2,1)} %gather_fusion) | copy-start | bytes 12582916 | tf_op jit(solution)/shard_map/while
  543.9 18.6 %copy-start.1 = (bf16[64,256,128]{2,1,0:T(8,128)(2,1)S(1)}, bf16[64,256,128]{2,1,0:T(8,128)(2,1)}, u32[]{:S(2)}) copy-start(bf16[64,256,128]{2,1,0:T(8,128)(2,1)} %gather_fusion) | copy-start | bytes 12582916 | tf_op jit(solution)/shard_map/while
  579.9 18.6 %copy-start.1 = (bf16[64,256,128]{2,1,0:T(8,128)(2,1)S(1)}, bf16[64,256,128]{2,1,0:T(8,128)(2,1)}, u32[]{:S(2)}) copy-start(bf16[64,256,128]{2,1,0:T(8,128)(2,1)} %gather_fusion) | copy-start | bytes 12582916 | tf_op jit(solution)/shard_map/while
  615.9 18.6 %copy-start.1 = (bf16[64,256,128]{2,1,0:T(8,128)(2,1)S(1)}, bf16[64,256,128]{2,1,0:T(8,128)(2,1)}, u32[]{:S(2)}) copy-start(bf16[64,256,128]{2,1,0:T(8,128)(2,1)} %gather_fusion) | copy-start | bytes 12582916 | tf_op jit(solution)/shard_map/while
  651.8 18.6 %copy-start.1 = (bf16[64,256,128]{2,1,0:T(8,128)(2,1)S(1)}, bf16[64,256,128]{2,1,0:T(8,128)(2,1)}, u32[]{:S(2)}) copy-start(bf16[64,256,128]{2,1,0:T(8,128)(2,1)} %gather_fusion) | copy-start | bytes 12582916 | tf_op jit(solution)/shard_map/while
  687.8 18.6 %copy-start.1 = (bf16[64,256,128]{2,1,0:T(8,128)(2,1)S(1)}, bf16[64,256,128]{2,1,0:T(8,128)(2,1)}, u32[]{:S(2)}) copy-start(bf16[64,256,128]{2,1,0:T(8,128)(2,1)} %gather_fusion) | copy-start | bytes 12582916 | tf_op jit(solution)/shard_map/while
  714.0 1.0 copy-start.2
Sparse Core Ops, SparseCore 0:
  9.5 129.1 all-gather.1
where the time goes:
time: 724 us; the launch traced here: 722 us
  matrix products  289 us (40%)
  local copies, waits for them, and re-layouts  152 us (21%)
  other arithmetic  142 us (20%)
  waiting for transfers between devices  124 us (17%)
  between operations  13.4 us (2%)
    dot_general x16, matrix products, attend_tile(): jnp.dot(tile_query, tile_keys.T, preferred_element_type=jnp.float32)  167 us
    gather x16, local copies, waits for them, and re-layouts, one_tile(): stored = source[chosen].reshape(-1, channels)  142 us
    reduce_sum x16, other arithmetic, attend_tile(): totals = jnp.sum(raised, axis=1, keepdims=True)  130 us
    all_gather x1, waiting for transfers between devices, body(): source = lax.all_gather(target, 'band', axis=0, tiled=True)  124 us
    dot_general x16, matrix products, attend_tile(): jnp.dot(weights, tile_keys, preferred_element_type=jnp.float32)  122 us
  transfers between devices with their start and end apart: 1, of which 1 were waited for; matrix products, arithmetic and copies ran while one was open for 1% of the time, Pallas kernels for 0%

commit v1 on v0

--- a/solution.py
+++ b/solution.py
@@ -3,6 +3,12 @@
 import jax.numpy as jnp
 from jax import lax
 from jax.sharding import PartitionSpec as P
+
+
+def refer_the_masks(mine, where_dim):
+    shaped = list(mine.shape[1:])
+    shaped[where_dim] *= mine.shape[0]
+    return jnp.moveaxis(mine, 0, where_dim).reshape(shaped)
 
 
 def attend_tile(tile_query, tile_keys, keep_mask):
@@ -22,7 +28,23 @@
 def body(query_tiles, target, tile_home, candidates, valid_mask):
     channels = target.shape[2]
     stored_rows = tile_home[candidates]
-    source = lax.all_gather(target, "band", axis=0, tiled=True)
+    n = lax.psum(1, "band")
+    heap = [(nth, (nth + 1) % n) for nth in range(n)]
+    r1, plain = ([], [])
+    t = 0
+    cards = [(ii, it) for it, ii in heap]
+    while t < n - 1:
+        if t % 2 == 0:
+            r1.append(lax.ppermute(r1[-1] if r1 else target, "band", heap))
+        else:
+            block_last = lax.ppermute(plain[-1] if plain else target, "band", cards)
+            plain.append(block_last)
+        t = t + 1
+    opened = jnp.stack([*r1[::-1], target, *plain])
+    formed = lax.axis_index("band")
+    r2 = formed - len(r1)
+    opened = opened[(jnp.arange(n) - r2) % n]
+    source = refer_the_masks(opened, 0)
 
     def one_tile(packed):
         tile_query, chosen, keep_mask = packed

time: 724 us -> 810 us (1.12)
  the two profiles are of different devices: /device:TPU:0 before, /device:TPU:1 now
where the time goes in v1:
time: 810 us; the launch traced here: 808 us
  matrix products  289 us (36%)
  local copies, waits for them, and re-layouts  198 us (24%)
  waiting for transfers between devices  157 us (19%)
  other arithmetic  142 us (18%)
  starting transfers between devices  21.2 us (3%)
    dot_general x16, matrix products, attend_tile(): jnp.dot(tile_query, tile_keys.T, preferred_element_type=jnp.float32)  167 us
    gather x16, local copies, waits for them, and re-layouts, one_tile(): stored = source[chosen].reshape(-1, channels)  143 us
    reduce_sum x16, other arithmetic, attend_tile(): totals = jnp.sum(raised, axis=1, keepdims=True)  130 us
    dot_general x16, matrix products, attend_tile(): jnp.dot(weights, tile_keys, preferred_element_type=jnp.float32)  122 us
    ppermute x8, waiting for transfers between devices, body(): r1.append(lax.ppermute(r1[-1] if r1 else target, 'band', heap))  97.7 us
    ppermute x7, waiting for transfers between devices, body(): block_last = lax.ppermute(plain[-1] if plain else target, 'band', cards)  59.5 us
    unnamed x47, local copies, waits for them, and re-layouts  32.1 us
    ppermute x8, starting transfers between devices, body(): r1.append(lax.ppermute(r1[-1] if r1 else target, 'band', heap))  20 us
  transfers between devices with their start and end apart: 15, of which 14 were waited for; matrix products, arithmetic and copies ran while one was open for 4% of the time, Pallas kernels for 0%

profile of v1, /device:TPU:1, one launch (start us, length us, event | category | flops | bytes accessed | tf_op | source)
XLA Modules:
  0.0 808.3 jit_solution(2296152881098622929)
XLA Ops:
  2.6 12.1 %collective-permute-done = bf16[16,256,128]{2,1,0:T(8,128)(2,1)S(1)} collective-permute-done((bf16[16,256,128]{2,1,0:T(8,128)(2,1)}, bf16[16,256,128]{2,1,0:T(8,128)(2,1)S(1)}, u32[]{:S(2)}, u32[]{:S(2)}) %collective-permute-start) | collective-permute-done | bytes 1048608 | tf_op jit(solution)/shard_map/ppermute | solution.py:38
  18.2 21.8 %collective-permute-done.1 = bf16[16,256,128]{2,1,0:T(8,128)(2,1)S(1)} collective-permute-done((bf16[16,256,128]{2,1,0:T(8,128)(2,1)S(1)}, bf16[16,256,128]{2,1,0:T(8,128)(2,1)S(1)}, u32[]{:S(2)}, u32[]{:S(2)}) %collective-permute-start.1) | collective-permute-done | bytes 1048608 | tf_op jit(solution)/shard_map/ppermute | solution.py:38
  42.5 11.4 %collective-permute-done.8 = bf16[16,256,128]{2,1,0:T(8,128)(2,1)S(1)} collective-permute-done((bf16[16,256,128]{2,1,0:T(8,128)(2,1)}, bf16[16,256,128]{2,1,0:T(8,128)(2,1)S(1)}, u32[]{:S(2)}, u32[]{:S(2)}) %collective-permute-start.8) | collective-permute-done | bytes 1048608 | tf_op jit(solution)/shard_map/ppermute | solution.py:40
  54.0 10.8 %collective-permute-done.2 = bf16[16,256,128]{2,1,0:T(8,128)(2,1)S(1)} collective-permute-done((bf16[16,256,128]{2,1,0:T(8,128)(2,1)S(1)}, bf16[16,256,128]{2,1,0:T(8,128)(2,1)S(1)}, u32[]{:S(2)}, u32[]{:S(2)}) %collective-permute-start.2) | collective-permute-done | bytes 1048608 | tf_op jit(solution)/shard_map/ppermute | solution.py:38
  67.2 12.2 %collective-permute-done.9 = bf16[16,256,128]{2,1,0:T(8,128)(2,1)S(1)} collective-permute-done((bf16[16,256,128]{2,1,0:T(8,128)(2,1)S(1)}, bf16[16,256,128]{2,1,0:T(8,128)(2,1)S(1)}, u32[]{:S(2)}, u32[]{:S(2)}) %collective-permute-start.9) | collective-permute-done | bytes 1048608 | tf_op jit(solution)/shard_map/ppermute | solution.py:40
  80.4 9.0 %collective-permute-done.3 = bf16[16,256,128]{2,1,0:T(8,128)(2,1)S(1)} collective-permute-done((bf16[16,256,128]{2,1,0:T(8,128)(2,1)S(1)}, bf16[16,256,128]{2,1,0:T(8,128)(2,1)S(1)}, u32[]{:S(2)}, u32[]{:S(2)}) %collective-permute-start.3) | collective-permute-done | bytes 1048608 | tf_op jit(solution)/shard_map/ppermute | solution.py:38
  92.0 11.6 %collective-permute-done.10 = bf16[16,256,128]{2,1,0:T(8,128)(2,1)S(1)} collective-permute-done((bf16[16,256,128]{2,1,0:T(8,128)(2,1)S(1)}, bf16[16,256,128]{2,1,0:T(8,128)(2,1)S(1)}, u32[]{:S(2)}, u32[]{:S(2)}) %collective-permute-start.10) | collective-permute-done | bytes 1048608 | tf_op jit(solution)/shard_map/ppermute | solution.py:40
  104.6 9.7 %collective-permute-done.4 = bf16[16,256,128]{2,1,0:T(8,128)(2,1)S(1)} collective-permute-done((bf16[16,256,128]{2,1,0:T(8,128)(2,1)S(1)}, bf16[16,256,128]{2,1,0:T(8,128)(2,1)S(1)}, u32[]{:S(2)}, u32[]{:S(2)}) %collective-permute-start.4) | collective-permute-done | bytes 1048608 | tf_op jit(solution)/shard_map/ppermute | solution.py:38
  116.7 10.2 %collective-permute-done.11 = bf16[16,256,128]{2,1,0:T(8,128)(2,1)S(1)} collective-permute-done((bf16[16,256,128]{2,1,0:T(8,128)(2,1)S(1)}, bf16[16,256,128]{2,1,0:T(8,128)(2,1)S(1)}, u32[]{:S(2)}, u32[]{:S(2)}) %collective-permute-start.11) | collective-permute-done | bytes 1048608 | tf_op jit(solution)/shard_map/ppermute | solution.py:40
  127.9 10.6 %collective-permute-done.5 = bf16[16,256,128]{2,1,0:T(8,128)(2,1)S(1)} collective-permute-done((bf16[16,256,128]{2,1,0:T(8,128)(2,1)S(1)}, bf16[16,256,128]{2,1,0:T(8,128)(2,1)S(1)}, u32[]{:S(2)}, u32[]{:S(2)}) %collective-permute-start.5) | collective-permute-done | bytes 1048608 | tf_op jit(solution)/shard_map/ppermute | solution.py:38
  141.0 10.5 %collective-permute-done.12 = bf16[16,256,128]{2,1,0:T(8,128)(2,1)} collective-permute-done((bf16[16,256,128]{2,1,0:T(8,128)(2,1)S(1)}, bf16[16,256,128]{2,1,0:T(8,128)(2,1)}, u32[]{:S(2)}, u32[]{:S(2)}) %collective-permute-start.12) | collective-permute-done | bytes 1048608 | tf_op jit(solution)/shard_map/ppermute | solution.py:40
  151.5 11.7 %collective-permute-done.6 = bf16[16,256,128]{2,1,0:T(8,128)(2,1)} collective-permute-done((bf16[16,256,128]{2,1,0:T(8,128)(2,1)S(1)}, bf16[16,256,128]{2,1,0:T(8,128)(2,1)}, u32[]{:S(2)}, u32[]{:S(2)}) %collective-permute-start.6) | collective-permute-done | bytes 1048608 | tf_op jit(solution)/shard_map/ppermute | solution.py:38
  177.1 12.0 %collective-permute-done.7 = bf16[16,256,128]{2,1,0:T(8,128)(2,1)} collective-permute-done((bf16[16,256,128]{2,1,0:T(8,128)(2,1)}, bf16[16,256,128]{2,1,0:T(8,128)(2,1)}, u32[]{:S(2)}, u32[]{:S(2)}) %collective-permute-start.7) | collective-permute-done | bytes 1048608 | tf_op jit(solution)/shard_map/ppermute | solution.py:38
  217.7 13.1 %gather_fusion.2 = bf16[16,16,256,128]{3,2,1,0:T(8,128)(2,1)} fusion(bf16[16,16,256,128]{3,2,1,0:T(8,128)(2,1)} %bitcast_dynamic-update-slice_fusion, s32[1024]{0:T(1024)S(1)} %pad_clamp_fusion.1), kind=kCustom, calls=%fused_computation.2 | custom fusion | bytes 33554496 | tf_op jit(solution)/shard_map/gather | solution.py:46
  230.8 575.8 %while.10 = (s32[]{:T(128)}, bf16[16,256,128]{2,1,0:T(8,128)(2,1)S(1)}, s32[16,64]{1,0:T(8,128)}, bf16[16,256,128]{2,1,0:T(8,128)(2,1)}, s32[16,64]{1,0:T(8,128)S(1)}, /*index=5*/bf16[256,256,128]{2,1,0:T(8,128)(2,1)}, s32[]{:T(128)}) while((s32[]{:T(128)}, bf16[16,256,128]{2,1,0:T(8,128)(2,1)S(1)}, s32[16,64]{1,0:T(8,128)}, ...), condition=%wide.region_3.4_spmd, body=%wide.region_0.3_spmd.sunk | while | flops 2181071616 | bytes 84093936 | solution.py:54
  230.8 8.9 %gather_fusion = bf16[64,256,128]{2,1,0:T(8,128)(2,1)} fusion(bf16[256,256,128]{2,1,0:T(8,128)(2,1)} %get-tuple-element.112, s32[1024]{0:T(1024)S(1)} %pad_clamp_fusion.3), kind=kCustom, calls=%fused_computation.clone.1 | custom fusion | bytes 8388864 | tf_op jit(solution)/shard_map/while/body/eval_jaxpr/gather | solution.py:51
  240.5 10.5 %fusion.25 = (f32[256]{0:T(256)S(1)}, f32[256,16384]{1,0:T(8,128)}) fusion(bf16[16384,128]{1,0:T(8,128)(2,1)} %bitcast.73, bf16[16,256,128]{2,1,0:T(8,128)(2,1)} %get-tuple-element.110, s32[]{:T(128)} %get-tuple-element.100, pred[16384]{0:T(1024)(128)(4,1)S(1)} %broadcast_in_dim.38), kind=kOutput, calls=%fused_computation.47.clone.1 | convolution fusion | flops 1086324480 | bytes 21054976 | tf_op jit(solution)/shard_map/while/body/eval_jaxpr/dot_general | solution.py:16
  251.0 8.1 %fusion.26 = f32[256]{0:T(256)S(1)} fusion(f32[256,16384]{1,0:T(8,128)} %get-tuple-element.91, f32[256]{0:T(256)S(1)} %get-tuple-element.92), kind=kLoop, calls=%fused_computation.7.clone.1 | loop fusion | flops 8388352 | bytes 16779264 | tf_op jit(solution)/shard_map/while/body/eval_jaxpr/reduce_sum | solution.py:23
  266.8 8.9 %gather_fusion = bf16[64,256,128]{2,1,0:T(8,128)(2,1)} fusion(bf16[256,256,128]{2,1,0:T(8,128)(2,1)} %get-tuple-element.112, s32[1024]{0:T(1024)S(1)} %pad_clamp_fusion.3), kind=kCustom, calls=%fused_computation.clone.1 | custom fusion | bytes 8388864 | tf_op jit(solution)/shard_map/while/body/eval_jaxpr/gather | solution.py:51
  276.5 10.5 %fusion.25 = (f32[256]{0:T(256)S(1)}, f32[256,16384]{1,0:T(8,128)}) fusion(bf16[16384,128]{1,0:T(8,128)(2,1)} %bitcast.73, bf16[16,256,128]{2,1,0:T(8,128)(2,1)} %get-tuple-element.110, s32[]{:T(128)} %get-tuple-element.100, pred[16384]{0:T(1024)(128)(4,1)S(1)} %broadcast_in_dim.38), kind=kOutput, calls=%fused_computation.47.clone.1 | convolution fusion | flops 1086324480 | bytes 21054976 | tf_op jit(solution)/shard_map/while/body/eval_jaxpr/dot_general | solution.py:16
  287.0 8.1 %fusion.26 = f32[256]{0:T(256)S(1)} fusion(f32[256,16384]{1,0:T(8,128)} %get-tuple-element.91, f32[256]{0:T(256)S(1)} %get-tuple-element.92), kind=kLoop, calls=%fused_computation.7.clone.1 | loop fusion | flops 8388352 | bytes 16779264 | tf_op jit(solution)/shard_map/while/body/eval_jaxpr/reduce_sum | solution.py:23
  295.1 7.6 fusion.27
  302.8 8.9 %gather_fusion = bf16[64,256,128]{2,1,0:T(8,128)(2,1)} fusion(bf16[256,256,128]{2,1,0:T(8,128)(2,1)} %get-tuple-element.112, s32[1024]{0:T(1024)S(1)} %pad_clamp_fusion.3), kind=kCustom, calls=%fused_computation.clone.1 | custom fusion | bytes 8388864 | tf_op jit(solution)/shard_map/while/body/eval_jaxpr/gather | solution.py:51
  312.5 10.5 %fusion.25 = (f32[256]{0:T(256)S(1)}, f32[256,16384]{1,0:T(8,128)}) fusion(bf16[16384,128]{1,0:T(8,128)(2,1)} %bitcast.73, bf16[16,256,128]{2,1,0:T(8,128)(2,1)} %get-tuple-element.110, s32[]{:T(128)} %get-tuple-element.100, pred[16384]{0:T(1024)(128)(4,1)S(1)} %broadcast_in_dim.38), kind=kOutput, calls=%fused_computation.47.clone.1 | convolution fusion | flops 1086324480 | bytes 21054976 | tf_op jit(solution)/shard_map/while/body/eval_jaxpr/dot_general | solution.py:16
  323.0 8.1 %fusion.26 = f32[256]{0:T(256)S(1)} fusion(f32[256,16384]{1,0:T(8,128)} %get-tuple-element.91, f32[256]{0:T(256)S(1)} %get-tuple-element.92), kind=kLoop, calls=%fused_computation.7.clone.1 | loop fusion | flops 8388352 | bytes 16779264 | tf_op jit(solution)/shard_map/while/body/eval_jaxpr/reduce_sum | solution.py:23
  338.8 8.9 %gather_fusion = bf16[64,256,128]{2,1,0:T(8,128)(2,1)} fusion(bf16[256,256,128]{2,1,0:T(8,128)(2,1)} %get-tuple-element.112, s32[1024]{0:T(1024)S(1)} %pad_clamp_fusion.3), kind=kCustom, calls=%fused_computation.clone.1 | custom fusion | bytes 8388864 | tf_op jit(solution)/shard_map/while/body/eval_jaxpr/gather | solution.py:51
  348.5 10.5 %fusion.25 = (f32[256]{0:T(256)S(1)}, f32[256,16384]{1,0:T(8,128)}) fusion(bf16[16384,128]{1,0:T(8,128)(2,1)} %bitcast.73, bf16[16,256,128]{2,1,0:T(8,128)(2,1)} %get-tuple-element.110, s32[]{:T(128)} %get-tuple-element.100, pred[16384]{0:T(1024)(128)(4,1)S(1)} %broadcast_in_dim.38), kind=kOutput, calls=%fused_computation.47.clone.1 | convolution fusion | flops 1086324480 | bytes 21054976 | tf_op jit(solution)/shard_map/while/body/eval_jaxpr/dot_general | solution.py:16
  359.0 8.1 %fusion.26 = f32[256]{0:T(256)S(1)} fusion(f32[256,16384]{1,0:T(8,128)} %get-tuple-element.91, f32[256]{0:T(256)S(1)} %get-tuple-element.92), kind=kLoop, calls=%fused_computation.7.clone.1 | loop fusion | flops 8388352 | bytes 16779264 | tf_op jit(solution)/shard_map/while/body/eval_jaxpr/reduce_sum | solution.py:23
  374.8 8.9 %gather_fusion = bf16[64,256,128]{2,1,0:T(8,128)(2,1)} fusion(bf16[256,256,128]{2,1,0:T(8,128)(2,1)} %get-tuple-element.112, s32[1024]{0:T(1024)S(1)} %pad_clamp_fusion.3), kind=kCustom, calls=%fused_computation.clone.1 | custom fusion | bytes 8388864 | tf_op jit(solution)/shard_map/while/body/eval_jaxpr/gather | solution.py:51
  384.5 10.5 %fusion.25 = (f32[256]{0:T(256)S(1)}, f32[256,16384]{1,0:T(8,128)}) fusion(bf16[16384,128]{1,0:T(8,128)(2,1)} %bitcast.73, bf16[16,256,128]{2,1,0:T(8,128)(2,1)} %get-tuple-element.110, s32[]{:T(128)} %get-tuple-element.100, pred[16384]{0:T(1024)(128)(4,1)S(1)} %broadcast_in_dim.38), kind=kOutput, calls=%fused_computation.47.clone.1 | convolution fusion | flops 1086324480 | bytes 21054976 | tf_op jit(solution)/shard_map/while/body/eval_jaxpr/dot_general | solution.py:16
  394.9 8.1 %fusion.26 = f32[256]{0:T(256)S(1)} fusion(f32[256,16384]{1,0:T(8,128)} %get-tuple-element.91, f32[256]{0:T(256)S(1)} %get-tuple-element.92), kind=kLoop, calls=%fused_computation.7.clone.1 | loop fusion | flops 8388352 | bytes 16779264 | tf_op jit(solution)/shard_map/while/body/eval_jaxpr/reduce_sum | solution.py:23
  410.8 8.9 %gather_fusion = bf16[64,256,128]{2,1,0:T(8,128)(2,1)} fusion(bf16[256,256,128]{2,1,0:T(8,128)(2,1)} %get-tuple-element.112, s32[1024]{0:T(1024)S(1)} %pad_clamp_fusion.3), kind=kCustom, calls=%fused_computation.clone.1 | custom fusion | bytes 8388864 | tf_op jit(solution)/shard_map/while/body/eval_jaxpr/gather | solution.py:51
  420.5 10.5 %fusion.25 = (f32[256]{0:T(256)S(1)}, f32[256,16384]{1,0:T(8,128)}) fusion(bf16[16384,128]{1,0:T(8,128)(2,1)} %bitcast.73, bf16[16,256,128]{2,1,0:T(8,128)(2,1)} %get-tuple-element.110, s32[]{:T(128)} %get-tuple-element.100, pred[16384]{0:T(1024)(128)(4,1)S(1)} %broadcast_in_dim.38), kind=kOutput, calls=%fused_computation.47.clone.1 | convolution fusion | flops 1086324480 | bytes 21054976 | tf_op jit(solution)/shard_map/while/body/eval_jaxpr/dot_general | solution.py:16
  430.9 8.1 %fusion.26 = f32[256]{0:T(256)S(1)} fusion(f32[256,16384]{1,0:T(8,128)} %get-tuple-element.91, f32[256]{0:T(256)S(1)} %get-tuple-element.92), kind=kLoop, calls=%fused_computation.7.clone.1 | loop fusion | flops 8388352 | bytes 16779264 | tf_op jit(solution)/shard_map/while/body/eval_jaxpr/reduce_sum | solution.py:23
  446.7 8.9 %gather_fusion = bf16[64,256,128]{2,1,0:T(8,128)(2,1)} fusion(bf16[256,256,128]{2,1,0:T(8,128)(2,1)} %get-tuple-element.112, s32[1024]{0:T(1024)S(1)} %pad_clamp_fusion.3), kind=kCustom, calls=%fused_computation.clone.1 | custom fusion | bytes 8388864 | tf_op jit(solution)/shard_map/while/body/eval_jaxpr/gather | solution.py:51
  456.5 10.5 %fusion.25 = (f32[256]{0:T(256)S(1)}, f32[256,16384]{1,0:T(8,128)}) fusion(bf16[16384,128]{1,0:T(8,128)(2,1)} %bitcast.73, bf16[16,256,128]{2,1,0:T(8,128)(2,1)} %get-tuple-element.110, s32[]{:T(128)} %get-tuple-element.100, pred[16384]{0:T(1024)(128)(4,1)S(1)} %broadcast_in_dim.38), kind=kOutput, calls=%fused_computation.47.clone.1 | convolution fusion | flops 1086324480 | bytes 21054976 | tf_op jit(solution)/shard_map/while/body/eval_jaxpr/dot_general | solution.py:16
  466.9 8.1 %fusion.26 = f32[256]{0:T(256)S(1)} fusion(f32[256,16384]{1,0:T(8,128)} %get-tuple-element.91, f32[256]{0:T(256)S(1)} %get-tuple-element.92), kind=kLoop, calls=%fused_computation.7.clone.1 | loop fusion | flops 8388352 | bytes 16779264 | tf_op jit(solution)/shard_map/while/body/eval_jaxpr/reduce_sum | solution.py:23
  482.7 8.9 %gather_fusion = bf16[64,256,128]{2,1,0:T(8,128)(2,1)} fusion(bf16[256,256,128]{2,1,0:T(8,128)(2,1)} %get-tuple-element.112, s32[1024]{0:T(1024)S(1)} %pad_clamp_fusion.3), kind=kCustom, calls=%fused_computation.clone.1 | custom fusion | bytes 8388864 | tf_op jit(solution)/shard_map/while/body/eval_jaxpr/gather | solution.py:51
  492.5 10.5 %fusion.25 = (f32[256]{0:T(256)S(1)}, f32[256,16384]{1,0:T(8,128)}) fusion(bf16[16384,128]{1,0:T(8,128)(2,1)} %bitcast.73, bf16[16,256,128]{2,1,0:T(8,128)(2,1)} %get-tuple-element.110, s32[]{:T(128)} %get-tuple-element.100, pred[16384]{0:T(1024)(128)(4,1)S(1)} %broadcast_in_dim.38), kind=kOutput, calls=%fused_computation.47.clone.1 | convolution fusion | flops 1086324480 | bytes 21054976 | tf_op jit(solution)/shard_map/while/body/eval_jaxpr/dot_general | solution.py:16
  502.9 8.1 %fusion.26 = f32[256]{0:T(256)S(1)} fusion(f32[256,16384]{1,0:T(8,128)} %get-tuple-element.91, f32[256]{0:T(256)S(1)} %get-tuple-element.92), kind=kLoop, calls=%fused_computation.7.clone.1 | loop fusion | flops 8388352 | bytes 16779264 | tf_op jit(solution)/shard_map/while/body/eval_jaxpr/reduce_sum | solution.py:23
  518.7 8.9 %gather_fusion = bf16[64,256,128]{2,1,0:T(8,128)(2,1)} fusion(bf16[256,256,128]{2,1,0:T(8,128)(2,1)} %get-tuple-element.112, s32[1024]{0:T(1024)S(1)} %pad_clamp_fusion.3), kind=kCustom, calls=%fused_computation.clone.1 | custom fusion | bytes 8388864 | tf_op jit(solution)/shard_map/while/body/eval_jaxpr/gather | solution.py:51
  528.5 10.5 %fusion.25 = (f32[256]{0:T(256)S(1)}, f32[256,16384]{1,0:T(8,128)}) fusion(bf16[16384,128]{1,0:T(8,128)(2,1)} %bitcast.73, bf16[16,256,128]{2,1,0:T(8,128)(2,1)} %get-tuple-element.110, s32[]{:T(128)} %get-tuple-element.100, pred[16384]{0:T(1024)(128)(4,1)S(1)} %broadcast_in_dim.38), kind=kOutput, calls=%fused_computation.47.clone.1 | convolution fusion | flops 1086324480 | bytes 21054976 | tf_op jit(solution)/shard_map/while/body/eval_jaxpr/dot_general | solution.py:16
  538.9 8.1 %fusion.26 = f32[256]{0:T(256)S(1)} fusion(f32[256,16384]{1,0:T(8,128)} %get-tuple-element.91, f32[256]{0:T(256)S(1)} %get-tuple-element.92), kind=kLoop, calls=%fused_computation.7.clone.1 | loop fusion | flops 8388352 | bytes 16779264 | tf_op jit(solution)/shard_map/while/body/eval_jaxpr/reduce_sum | solution.py:23
  554.7 8.9 %gather_fusion = bf16[64,256,128]{2,1,0:T(8,128)(2,1)} fusion(bf16[256,256,128]{2,1,0:T(8,128)(2,1)} %get-tuple-element.112, s32[1024]{0:T(1024)S(1)} %pad_clamp_fusion.3), kind=kCustom, calls=%fused_computation.clone.1 | custom fusion | bytes 8388864 | tf_op jit(solution)/shard_map/while/body/eval_jaxpr/gather | solution.py:51
  564.5 10.5 %fusion.25 = (f32[256]{0:T(256)S(1)}, f32[256,16384]{1,0:T(8,128)}) fusion(bf16[16384,128]{1,0:T(8,128)(2,1)} %bitcast.73, bf16[16,256,128]{2,1,0:T(8,128)(2,1)} %get-tuple-element.110, s32[]{:T(128)} %get-tuple-element.100, pred[16384]{0:T(1024)(128)(4,1)S(1)} %broadcast_in_dim.38), kind=kOutput, calls=%fused_computation.47.clone.1 | convolution fusion | flops 1086324480 | bytes 21054976 | tf_op jit(solution)/shard_map/while/body/eval_jaxpr/dot_general | solution.py:16
  574.9 8.1 %fusion.26 = f32[256]{0:T(256)S(1)} fusion(f32[256,16384]{1,0:T(8,128)} %get-tuple-element.91, f32[256]{0:T(256)S(1)} %get-tuple-element.92), kind=kLoop, calls=%fused_computation.7.clone.1 | loop fusion | flops 8388352 | bytes 16779264 | tf_op jit(solution)/shard_map/while/body/eval_jaxpr/reduce_sum | solution.py:23
  590.7 8.9 %gather_fusion = bf16[64,256,128]{2,1,0:T(8,128)(2,1)} fusion(bf16[256,256,128]{2,1,0:T(8,128)(2,1)} %get-tuple-element.112, s32[1024]{0:T(1024)S(1)} %pad_clamp_fusion.3), kind=kCustom, calls=%fused_computation.clone.1 | custom fusion | bytes 8388864 | tf_op jit(solution)/shard_map/while/body/eval_jaxpr/gather | solution.py:51
  600.4 10.5 %fusion.25 = (f32[256]{0:T(256)S(1)}, f32[256,16384]{1,0:T(8,128)}) fusion(bf16[16384,128]{1,0:T(8,128)(2,1)} %bitcast.73, bf16[16,256,128]{2,1,0:T(8,128)(2,1)} %get-tuple-element.110, s32[]{:T(128)} %get-tuple-element.100, pred[16384]{0:T(1024)(128)(4,1)S(1)} %broadcast_in_dim.38), kind=kOutput, calls=%fused_computation.47.clone.1 | convolution fusion | flops 1086324480 | bytes 21054976 | tf_op jit(solution)/shard_map/while/body/eval_jaxpr/dot_general | solution.py:16
  610.9 8.1 %fusion.26 = f32[256]{0:T(256)S(1)} fusion(f32[256,16384]{1,0:T(8,128)} %get-tuple-element.91, f32[256]{0:T(256)S(1)} %get-tuple-element.92), kind=kLoop, calls=%fused_computation.7.clone.1 | loop fusion | flops 8388352 | bytes 16779264 | tf_op jit(solution)/shard_map/while/body/eval_jaxpr/reduce_sum | solution.py:23
  626.7 8.9 %gather_fusion = bf16[64,256,128]{2,1,0:T(8,128)(2,1)} fusion(bf16[256,256,128]{2,1,0:T(8,128)(2,1)} %get-tuple-element.112, s32[1024]{0:T(1024)S(1)} %pad_clamp_fusion.3), kind=kCustom, calls=%fused_computation.clone.1 | custom fusion | bytes 8388864 | tf_op jit(solution)/shard_map/while/body/eval_jaxpr/gather | solution.py:51
  636.4 10.5 %fusion.25 = (f32[256]{0:T(256)S(1)}, f32[256,16384]{1,0:T(8,128)}) fusion(bf16[16384,128]{1,0:T(8,128)(2,1)} %bitcast.73, bf16[16,256,128]{2,1,0:T(8,128)(2,1)} %get-tuple-element.110, s32[]{:T(128)} %get-tuple-element.100, pred[16384]{0:T(1024)(128)(4,1)S(1)} %broadcast_in_dim.38), kind=kOutput, calls=%fused_computation.47.clone.1 | convolution fusion | flops 1086324480 | bytes 21054976 | tf_op jit(solution)/shard_map/while/body/eval_jaxpr/dot_general | solution.py:16
  646.9 8.1 %fusion.26 = f32[256]{0:T(256)S(1)} fusion(f32[256,16384]{1,0:T(8,128)} %get-tuple-element.91, f32[256]{0:T(256)S(1)} %get-tuple-element.92), kind=kLoop, calls=%fused_computation.7.clone.1 | loop fusion | flops 8388352 | bytes 16779264 | tf_op jit(solution)/shard_map/while/body/eval_jaxpr/reduce_sum | solution.py:23
  662.7 8.9 %gather_fusion = bf16[64,256,128]{2,1,0:T(8,128)(2,1)} fusion(bf16[256,256,128]{2,1,0:T(8,128)(2,1)} %get-tuple-element.112, s32[1024]{0:T(1024)S(1)} %pad_clamp_fusion.3), kind=kCustom, calls=%fused_computation.clone.1 | custom fusion | bytes 8388864 | tf_op jit(solution)/shard_map/while/body/eval_jaxpr/gather | solution.py:51
  672.4 10.5 %fusion.25 = (f32[256]{0:T(256)S(1)}, f32[256,16384]{1,0:T(8,128)}) fusion(bf16[16384,128]{1,0:T(8,128)(2,1)} %bitcast.73, bf16[16,256,128]{2,1,0:T(8,128)(2,1)} %get-tuple-element.110, s32[]{:T(128)} %get-tuple-element.100, pred[16384]{0:T(1024)(128)(4,1)S(1)} %broadcast_in_dim.38), kind=kOutput, calls=%fused_computation.47.clone.1 | convolution fusion | flops 1086324480 | bytes 21054976 | tf_op jit(solution)/shard_map/while/body/eval_jaxpr/dot_general | solution.py:16
  682.9 8.1 %fusion.26 = f32[256]{0:T(256)S(1)} fusion(f32[256,16384]{1,0:T(8,128)} %get-tuple-element.91, f32[256]{0:T(256)S(1)} %get-tuple-element.92), kind=kLoop, calls=%fused_computation.7.clone.1 | loop fusion | flops 8388352 | bytes 16779264 | tf_op jit(solution)/shard_map/while/body/eval_jaxpr/reduce_sum | solution.py:23
  698.7 8.9 %gather_fusion = bf16[64,256,128]{2,1,0:T(8,128)(2,1)} fusion(bf16[256,256,128]{2,1,0:T(8,128)(2,1)} %get-tuple-element.112, s32[1024]{0:T(1024)S(1)} %pad_clamp_fusion.3), kind=kCustom, calls=%fused_computation.clone.1 | custom fusion | bytes 8388864 | tf_op jit(solution)/shard_map/while/body/eval_jaxpr/gather | solution.py:51
  708.4 10.5 %fusion.25 = (f32[256]{0:T(256)S(1)}, f32[256,16384]{1,0:T(8,128)}) fusion(bf16[16384,128]{1,0:T(8,128)(2,1)} %bitcast.73, bf16[16,256,128]{2,1,0:T(8,128)(2,1)} %get-tuple-element.110, s32[]{:T(128)} %get-tuple-element.100, pred[16384]{0:T(1024)(128)(4,1)S(1)} %broadcast_in_dim.38), kind=kOutput, calls=%fused_computation.47.clone.1 | convolution fusion | flops 1086324480 | bytes 21054976 | tf_op jit(solution)/shard_map/while/body/eval_jaxpr/dot_general | solution.py:16
  718.9 8.1 %fusion.26 = f32[256]{0:T(256)S(1)} fusion(f32[256,16384]{1,0:T(8,128)} %get-tuple-element.91, f32[256]{0:T(256)S(1)} %get-tuple-element.92), kind=kLoop, calls=%fused_computation.7.clone.1 | loop fusion | flops 8388352 | bytes 16779264 | tf_op jit(solution)/shard_map/while/body/eval_jaxpr/reduce_sum | solution.py:23
  734.7 8.9 %gather_fusion = bf16[64,256,128]{2,1,0:T(8,128)(2,1)} fusion(bf16[256,256,128]{2,1,0:T(8,128)(2,1)} %get-tuple-element.112, s32[1024]{0:T(1024)S(1)} %pad_clamp_fusion.3), kind=kCustom, calls=%fused_computation.clone.1 | custom fusion | bytes 8388864 | tf_op jit(solution)/shard_map/while/body/eval_jaxpr/gather | solution.py:51
  744.4 10.5 %fusion.25 = (f32[256]{0:T(256)S(1)}, f32[256,16384]{1,0:T(8,128)}) fusion(bf16[16384,128]{1,0:T(8,128)(2,1)} %bitcast.73, bf16[16,256,128]{2,1,0:T(8,128)(2,1)} %get-tuple-element.110, s32[]{:T(128)} %get-tuple-element.100, pred[16384]{0:T(1024)(128)(4,1)S(1)} %broadcast_in_dim.38), kind=kOutput, calls=%fused_computation.47.clone.1 | convolution fusion | flops 1086324480 | bytes 21054976 | tf_op jit(solution)/shard_map/while/body/eval_jaxpr/dot_general | solution.py:16
  754.9 8.1 %fusion.26 = f32[256]{0:T(256)S(1)} fusion(f32[256,16384]{1,0:T(8,128)} %get-tuple-element.91, f32[256]{0:T(256)S(1)} %get-tuple-element.92), kind=kLoop, calls=%fused_computation.7.clone.1 | loop fusion | flops 8388352 | bytes 16779264 | tf_op jit(solution)/shard_map/while/body/eval_jaxpr/reduce_sum | solution.py:23
  770.7 8.9 %gather_fusion = bf16[64,256,128]{2,1,0:T(8,128)(2,1)} fusion(bf16[256,256,128]{2,1,0:T(8,128)(2,1)} %get-tuple-element.112, s32[1024]{0:T(1024)S(1)} %pad_clamp_fusion.3), kind=kCustom, calls=%fused_computation.clone.1 | custom fusion | bytes 8388864 | tf_op jit(solution)/shard_map/while/body/eval_jaxpr/gather | solution.py:51
  780.4 10.5 %fusion.25 = (f32[256]{0:T(256)S(1)}, f32[256,16384]{1,0:T(8,128)}) fusion(bf16[16384,128]{1,0:T(8,128)(2,1)} %bitcast.73, bf16[16,256,128]{2,1,0:T(8,128)(2,1)} %get-tuple-element.110, s32[]{:T(128)} %get-tuple-element.100, pred[16384]{0:T(1024)(128)(4,1)S(1)} %broadcast_in_dim.38), kind=kOutput, calls=%fused_computation.47.clone.1 | convolution fusion | flops 1086324480 | bytes 21054976 | tf_op jit(solution)/shard_map/while/body/eval_jaxpr/dot_general | solution.py:16
  790.9 8.1 %fusion.26 = f32[256]{0:T(256)S(1)} fusion(f32[256,16384]{1,0:T(8,128)} %get-tuple-element.91, f32[256]{0:T(256)S(1)} %get-tuple-element.92), kind=kLoop, calls=%fused_computation.7.clone.1 | loop fusion | flops 8388352 | bytes 16779264 | tf_op jit(solution)/shard_map/while/body/eval_jaxpr/reduce_sum | solution.py:23
  (200 shorter events, 192.6 us)
Async XLA Ops:
  0.0 166.6 %copy-start = (s32[256]{0:T(256)S(1)}, s32[256]{0:T(256)}, u32[]{:S(2)}) copy-start(s32[256]{0:T(256)} %param.9) | copy-start | bytes 3076
  0.0 206.5 %copy-start.3 = (bf16[16,256,128]{2,1,0:T(8,128)(2,1)S(1)}, bf16[16,256,128]{2,1,0:T(8,128)(2,1)}, u32[]{:S(2)}) copy-start(bf16[16,256,128]{2,1,0:T(8,128)(2,1)} %param.8) | copy-start | bytes 3145732
  0.0 14.7 %collective-permute-start = (bf16[16,256,128]{2,1,0:T(8,128)(2,1)}, bf16[16,256,128]{2,1,0:T(8,128)(2,1)S(1)}, u32[]{:S(2)}, u32[]{:S(2)}) collective-permute-start(bf16[16,256,128]{2,1,0:T(8,128)(2,1)} %param.8), channel_id=1, source_target_pairs={{0,1},{1,2},{2,3},{3,4},{4,5},{5,6},{6,7},{7,8},{8,9},{9,10},{10,1... | collective-permute-start | bytes 3145736 | tf_op jit(solution)/shard_map/ppermute | solution.py:38
  14.7 25.4 %collective-permute-start.1 = (bf16[16,256,128]{2,1,0:T(8,128)(2,1)S(1)}, bf16[16,256,128]{2,1,0:T(8,128)(2,1)S(1)}, u32[]{:S(2)}, u32[]{:S(2)}) collective-permute-start(bf16[16,256,128]{2,1,0:T(8,128)(2,1)S(1)} %collective-permute-done), channel_id=1, source_target_pairs={{0,1},{1,2},{2,3},{3,4},{4,5},{5,6},{6,7},{7,8},{8,9},{9,10},{10,1... | collective-permute-start | bytes 3145736 | tf_op jit(solution)/shard_map/ppermute | solution.py:38
  17.1 36.9 %collective-permute-start.8 = (bf16[16,256,128]{2,1,0:T(8,128)(2,1)}, bf16[16,256,128]{2,1,0:T(8,128)(2,1)S(1)}, u32[]{:S(2)}, u32[]{:S(2)}) collective-permute-start(bf16[16,256,128]{2,1,0:T(8,128)(2,1)} %param.8), channel_id=1, source_target_pairs={{1,0},{2,1},{3,2},{4,3},{5,4},{6,5},{7,6},{8,7},{9,8},{10,9},{11,1... | collective-permute-start | bytes 3145736 | tf_op jit(solution)/shard_map/ppermute | solution.py:40
  40.0 39.4 %copy-start.4 = (bf16[16,256,128]{2,1,0:T(8,128)(2,1)}, bf16[16,256,128]{2,1,0:T(8,128)(2,1)S(1)}, u32[]{:S(2)}) copy-start(bf16[16,256,128]{2,1,0:T(8,128)(2,1)S(1)} %collective-permute-done.1) | copy-start | bytes 3145732
  40.0 24.7 %collective-permute-start.2 = (bf16[16,256,128]{2,1,0:T(8,128)(2,1)S(1)}, bf16[16,256,128]{2,1,0:T(8,128)(2,1)S(1)}, u32[]{:S(2)}, u32[]{:S(2)}) collective-permute-start(bf16[16,256,128]{2,1,0:T(8,128)(2,1)S(1)} %collective-permute-done.1), channel_id=1, source_target_pairs={{0,1},{1,2},{2,3},{3,4},{4,5},{5,6},{6,7},{7,8},{8,9},{9,10},{10,1... | collective-permute-start | bytes 3145736 | tf_op jit(solution)/shard_map/ppermute | solution.py:38
  54.0 25.5 %collective-permute-start.9 = (bf16[16,256,128]{2,1,0:T(8,128)(2,1)S(1)}, bf16[16,256,128]{2,1,0:T(8,128)(2,1)S(1)}, u32[]{:S(2)}, u32[]{:S(2)}) collective-permute-start(bf16[16,256,128]{2,1,0:T(8,128)(2,1)S(1)} %collective-permute-done.8), channel_id=1, source_target_pairs={{1,0},{2,1},{3,2},{4,3},{5,4},{6,5},{7,6},{8,7},{9,8},{10,9},{11,1... | collective-permute-start | bytes 3145736 | tf_op jit(solution)/shard_map/ppermute | solution.py:40
  64.7 38.9 %copy-start.7 = (bf16[16,256,128]{2,1,0:T(8,128)(2,1)}, bf16[16,256,128]{2,1,0:T(8,128)(2,1)S(1)}, u32[]{:S(2)}) copy-start(bf16[16,256,128]{2,1,0:T(8,128)(2,1)S(1)} %collective-permute-done.2) | copy-start | bytes 3145732
  64.7 24.7 %collective-permute-start.3 = (bf16[16,256,128]{2,1,0:T(8,128)(2,1)S(1)}, bf16[16,256,128]{2,1,0:T(8,128)(2,1)S(1)}, u32[]{:S(2)}, u32[]{:S(2)}) collective-permute-start(bf16[16,256,128]{2,1,0:T(8,128)(2,1)S(1)} %collective-permute-done.2), channel_id=1, source_target_pairs={{0,1},{1,2},{2,3},{3,4},{4,5},{5,6},{6,7},{7,8},{8,9},{9,10},{10,1... | collective-permute-start | bytes 3145736 | tf_op jit(solution)/shard_map/ppermute | solution.py:38
  79.4 1.0 copy-start.5
  79.4 24.2 %collective-permute-start.10 = (bf16[16,256,128]{2,1,0:T(8,128)(2,1)S(1)}, bf16[16,256,128]{2,1,0:T(8,128)(2,1)S(1)}, u32[]{:S(2)}, u32[]{:S(2)}) collective-permute-start(bf16[16,256,128]{2,1,0:T(8,128)(2,1)S(1)} %collective-permute-done.9), channel_id=1, source_target_pairs={{1,0},{2,1},{3,2},{4,3},{5,4},{6,5},{7,6},{8,7},{9,8},{10,9},{11,1... | collective-permute-start | bytes 3145736 | tf_op jit(solution)/shard_map/ppermute | solution.py:40
  89.5 62.0 %copy-start.12 = (bf16[16,256,128]{2,1,0:T(8,128)(2,1)}, bf16[16,256,128]{2,1,0:T(8,128)(2,1)S(1)}, u32[]{:S(2)}) copy-start(bf16[16,256,128]{2,1,0:T(8,128)(2,1)S(1)} %collective-permute-done.3) | copy-start | bytes 3145732
  89.5 24.7 %collective-permute-start.4 = (bf16[16,256,128]{2,1,0:T(8,128)(2,1)S(1)}, bf16[16,256,128]{2,1,0:T(8,128)(2,1)S(1)}, u32[]{:S(2)}, u32[]{:S(2)}) collective-permute-start(bf16[16,256,128]{2,1,0:T(8,128)(2,1)S(1)} %collective-permute-done.3), channel_id=1, source_target_pairs={{0,1},{1,2},{2,3},{3,4},{4,5},{5,6},{6,7},{7,8},{8,9},{9,10},{10,1... | collective-permute-start | bytes 3145736 | tf_op jit(solution)/shard_map/ppermute | solution.py:38
  103.6 1.0 copy-start.8
  103.6 23.3 %collective-permute-start.11 = (bf16[16,256,128]{2,1,0:T(8,128)(2,1)S(1)}, bf16[16,256,128]{2,1,0:T(8,128)(2,1)S(1)}, u32[]{:S(2)}, u32[]{:S(2)}) collective-permute-start(bf16[16,256,128]{2,1,0:T(8,128)(2,1)S(1)} %collective-permute-done.10), channel_id=1, source_target_pairs={{1,0},{2,1},{3,2},{4,3},{5,4},{6,5},{7,6},{8,7},{9,8},{10,9},{11,1... | collective-permute-start | bytes 3145736 | tf_op jit(solution)/shard_map/ppermute | solution.py:40
  114.2 37.3 %copy-start.13 = (bf16[16,256,128]{2,1,0:T(8,128)(2,1)}, bf16[16,256,128]{2,1,0:T(8,128)(2,1)S(1)}, u32[]{:S(2)}) copy-start(bf16[16,256,128]{2,1,0:T(8,128)(2,1)S(1)} %collective-permute-done.4) | copy-start | bytes 3145732
  114.2 24.3 %collective-permute-start.5 = (bf16[16,256,128]{2,1,0:T(8,128)(2,1)S(1)}, bf16[16,256,128]{2,1,0:T(8,128)(2,1)S(1)}, u32[]{:S(2)}, u32[]{:S(2)}) collective-permute-start(bf16[16,256,128]{2,1,0:T(8,128)(2,1)S(1)} %collective-permute-done.4), channel_id=1, source_target_pairs={{0,1},{1,2},{2,3},{3,4},{4,5},{5,6},{6,7},{7,8},{8,9},{9,10},{10,1... | collective-permute-start | bytes 3145736 | tf_op jit(solution)/shard_map/ppermute | solution.py:38
  126.9 1.0 copy-start.10
  127.9 23.6 %collective-permute-start.12 = (bf16[16,256,128]{2,1,0:T(8,128)(2,1)S(1)}, bf16[16,256,128]{2,1,0:T(8,128)(2,1)}, u32[]{:S(2)}, u32[]{:S(2)}) collective-permute-start(bf16[16,256,128]{2,1,0:T(8,128)(2,1)S(1)} %collective-permute-done.11), channel_id=1, source_target_pairs={{1,0},{2,1},{3,2},{4,3},{5,4},{6,5},{7,6},{8,7},{9,8},{10,9},{11,1... | collective-permute-start | bytes 3145736 | tf_op jit(solution)/shard_map/ppermute | solution.py:40
  138.6 24.7 %copy-start.14 = (bf16[16,256,128]{2,1,0:T(8,128)(2,1)}, bf16[16,256,128]{2,1,0:T(8,128)(2,1)S(1)}, u32[]{:S(2)}) copy-start(bf16[16,256,128]{2,1,0:T(8,128)(2,1)S(1)} %collective-permute-done.5) | copy-start | bytes 3145732
  138.6 24.7 %collective-permute-start.6 = (bf16[16,256,128]{2,1,0:T(8,128)(2,1)S(1)}, bf16[16,256,128]{2,1,0:T(8,128)(2,1)}, u32[]{:S(2)}, u32[]{:S(2)}) collective-permute-start(bf16[16,256,128]{2,1,0:T(8,128)(2,1)S(1)} %collective-permute-done.5), channel_id=1, source_target_pairs={{0,1},{1,2},{2,3},{3,4},{4,5},{5,6},{6,7},{7,8},{8,9},{9,10},{10,1... | collective-permute-start | bytes 3145736 | tf_op jit(solution)/shard_map/ppermute | solution.py:38
  151.5 25.6 %collective-permute-start.13 = (bf16[16,256,128]{2,1,0:T(8,128)(2,1)}, bf16[16,256,128]{2,1,0:T(8,128)(2,1)}, u32[]{:S(2)}, u32[]{:S(2)}) collective-permute-start(bf16[16,256,128]{2,1,0:T(8,128)(2,1)} %collective-permute-done.12), channel_id=1, source_target_pairs={{1,0},{2,1},{3,2},{4,3},{5,4},{6,5},{7,6},{8,7},{9,8},{10,9},{11,1... | collective-permute-start | bytes 3145736 | tf_op jit(solution)/shard_map/ppermute | solution.py:40
  163.2 25.9 %collective-permute-start.7 = (bf16[16,256,128]{2,1,0:T(8,128)(2,1)}, bf16[16,256,128]{2,1,0:T(8,128)(2,1)}, u32[]{:S(2)}, u32[]{:S(2)}) collective-permute-start(bf16[16,256,128]{2,1,0:T(8,128)(2,1)} %collective-permute-done.6), channel_id=1, source_target_pairs={{0,1},{1,2},{2,3},{3,4},{4,5},{5,6},{6,7},{7,8},{8,9},{9,10},{10,1... | collective-permute-start | bytes 3145736 | tf_op jit(solution)/shard_map/ppermute | solution.py:38
  173.5 35.2 %copy-start.6 = (bf16[16,256,128]{2,1,0:T(8,128)(2,1)S(1)}, bf16[16,256,128]{2,1,0:T(8,128)(2,1)}, u32[]{:S(2)}) copy-start(bf16[16,256,128]{2,1,0:T(8,128)(2,1)} %copy-done.5) | copy-start | bytes 3145732
  173.5 36.2 %copy-start.9 = (bf16[16,256,128]{2,1,0:T(8,128)(2,1)S(1)}, bf16[16,256,128]{2,1,0:T(8,128)(2,1)}, u32[]{:S(2)}) copy-start(bf16[16,256,128]{2,1,0:T(8,128)(2,1)} %copy-done.8) | copy-start | bytes 3145732
  173.5 37.3 %copy-start.11 = (bf16[16,256,128]{2,1,0:T(8,128)(2,1)S(1)}, bf16[16,256,128]{2,1,0:T(8,128)(2,1)}, u32[]{:S(2)}) copy-start(bf16[16,256,128]{2,1,0:T(8,128)(2,1)} %copy-done.10) | copy-start | bytes 3145732
  177.1 39.4 %collective-permute-start.14 = (bf16[16,256,128]{2,1,0:T(8,128)(2,1)}, bf16[16,256,128]{2,1,0:T(8,128)(2,1)S(1)}, u32[]{:S(2)}, u32[]{:S(2)}) collective-permute-start(bf16[16,256,128]{2,1,0:T(8,128)(2,1)} %collective-permute-done.13), channel_id=1, source_target_pairs={{1,0},{2,1},{3,2},{4,3},{5,4},{6,5},{7,6},{8,7},{9,8},{10,9},{11,1... | collective-permute-start | bytes 3145736 | tf_op jit(solution)/shard_map/ppermute | solution.py:40
  217.7 13.1 %copy-start.15 = (bf16[16,256,128]{2,1,0:T(8,128)(2,1)S(1)}, bf16[16,256,128]{2,1,0:T(8,128)(2,1)}, u32[]{:S(2)}) copy-start(bf16[16,256,128]{2,1,0:T(8,128)(2,1)} %custom-call.7) | copy-start | bytes 3145732
  240.5 18.6 %copy-start.2 = (bf16[64,256,128]{2,1,0:T(8,128)(2,1)S(1)}, bf16[64,256,128]{2,1,0:T(8,128)(2,1)}, u32[]{:S(2)}) copy-start(bf16[64,256,128]{2,1,0:T(8,128)(2,1)} %gather_fusion) | copy-start | bytes 12582916 | tf_op jit(solution)/shard_map/while
  276.5 18.6 %copy-start.2 = (bf16[64,256,128]{2,1,0:T(8,128)(2,1)S(1)}, bf16[64,256,128]{2,1,0:T(8,128)(2,1)}, u32[]{:S(2)}) copy-start(bf16[64,256,128]{2,1,0:T(8,128)(2,1)} %gather_fusion) | copy-start | bytes 12582916 | tf_op jit(solution)/shard_map/while
  312.5 18.6 %copy-start.2 = (bf16[64,256,128]{2,1,0:T(8,128)(2,1)S(1)}, bf16[64,256,128]{2,1,0:T(8,128)(2,1)}, u32[]{:S(2)}) copy-start(bf16[64,256,128]{2,1,0:T(8,128)(2,1)} %gather_fusion) | copy-start | bytes 12582916 | tf_op jit(solution)/shard_map/while
  348.5 18.6 %copy-start.2 = (bf16[64,256,128]{2,1,0:T(8,128)(2,1)S(1)}, bf16[64,256,128]{2,1,0:T(8,128)(2,1)}, u32[]{:S(2)}) copy-start(bf16[64,256,128]{2,1,0:T(8,128)(2,1)} %gather_fusion) | copy-start | bytes 12582916 | tf_op jit(solution)/shard_map/while
  384.5 18.6 %copy-start.2 = (bf16[64,256,128]{2,1,0:T(8,128)(2,1)S(1)}, bf16[64,256,128]{2,1,0:T(8,128)(2,1)}, u32[]{:S(2)}) copy-start(bf16[64,256,128]{2,1,0:T(8,128)(2,1)} %gather_fusion) | copy-start | bytes 12582916 | tf_op jit(solution)/shard_map/while
  420.5 18.6 %copy-start.2 = (bf16[64,256,128]{2,1,0:T(8,128)(2,1)S(1)}, bf16[64,256,128]{2,1,0:T(8,128)(2,1)}, u32[]{:S(2)}) copy-start(bf16[64,256,128]{2,1,0:T(8,128)(2,1)} %gather_fusion) | copy-start | bytes 12582916 | tf_op jit(solution)/shard_map/while
  456.5 18.6 %copy-start.2 = (bf16[64,256,128]{2,1,0:T(8,128)(2,1)S(1)}, bf16[64,256,128]{2,1,0:T(8,128)(2,1)}, u32[]{:S(2)}) copy-start(bf16[64,256,128]{2,1,0:T(8,128)(2,1)} %gather_fusion) | copy-start | bytes 12582916 | tf_op jit(solution)/shard_map/while
  492.5 18.6 %copy-start.2 = (bf16[64,256,128]{2,1,0:T(8,128)(2,1)S(1)}, bf16[64,256,128]{2,1,0:T(8,128)(2,1)}, u32[]{:S(2)}) copy-start(bf16[64,256,128]{2,1,0:T(8,128)(2,1)} %gather_fusion) | copy-start | bytes 12582916 | tf_op jit(solution)/shard_map/while
  528.4 18.6 %copy-start.2 = (bf16[64,256,128]{2,1,0:T(8,128)(2,1)S(1)}, bf16[64,256,128]{2,1,0:T(8,128)(2,1)}, u32[]{:S(2)}) copy-start(bf16[64,256,128]{2,1,0:T(8,128)(2,1)} %gather_fusion) | copy-start | bytes 12582916 | tf_op jit(solution)/shard_map/while
  564.4 18.6 %copy-start.2 = (bf16[64,256,128]{2,1,0:T(8,128)(2,1)S(1)}, bf16[64,256,128]{2,1,0:T(8,128)(2,1)}, u32[]{:S(2)}) copy-start(bf16[64,256,128]{2,1,0:T(8,128)(2,1)} %gather_fusion) | copy-start | bytes 12582916 | tf_op jit(solution)/shard_map/while
  600.4 18.6 %copy-start.2 = (bf16[64,256,128]{2,1,0:T(8,128)(2,1)S(1)}, bf16[64,256,128]{2,1,0:T(8,128)(2,1)}, u32[]{:S(2)}) copy-start(bf16[64,256,128]{2,1,0:T(8,128)(2,1)} %gather_fusion) | copy-start | bytes 12582916 | tf_op jit(solution)/shard_map/while
  636.4 18.6 %copy-start.2 = (bf16[64,256,128]{2,1,0:T(8,128)(2,1)S(1)}, bf16[64,256,128]{2,1,0:T(8,128)(2,1)}, u32[]{:S(2)}) copy-start(bf16[64,256,128]{2,1,0:T(8,128)(2,1)} %gather_fusion) | copy-start | bytes 12582916 | tf_op jit(solution)/shard_map/while
  672.4 18.6 %copy-start.2 = (bf16[64,256,128]{2,1,0:T(8,128)(2,1)S(1)}, bf16[64,256,128]{2,1,0:T(8,128)(2,1)}, u32[]{:S(2)}) copy-start(bf16[64,256,128]{2,1,0:T(8,128)(2,1)} %gather_fusion) | copy-start | bytes 12582916 | tf_op jit(solution)/shard_map/while
  708.4 18.6 %copy-start.2 = (bf16[64,256,128]{2,1,0:T(8,128)(2,1)S(1)}, bf16[64,256,128]{2,1,0:T(8,128)(2,1)}, u32[]{:S(2)}) copy-start(bf16[64,256,128]{2,1,0:T(8,128)(2,1)} %gather_fusion) | copy-start | bytes 12582916 | tf_op jit(solution)/shard_map/while
  744.4 18.6 %copy-start.2 = (bf16[64,256,128]{2,1,0:T(8,128)(2,1)S(1)}, bf16[64,256,128]{2,1,0:T(8,128)(2,1)}, u32[]{:S(2)}) copy-start(bf16[64,256,128]{2,1,0:T(8,128)(2,1)} %gather_fusion) | copy-start | bytes 12582916 | tf_op jit(solution)/shard_map/while
  780.4 18.6 %copy-start.2 = (bf16[64,256,128]{2,1,0:T(8,128)(2,1)S(1)}, bf16[64,256,128]{2,1,0:T(8,128)(2,1)}, u32[]{:S(2)}) copy-start(bf16[64,256,128]{2,1,0:T(8,128)(2,1)} %gather_fusion) | copy-start | bytes 12582916 | tf_op jit(solution)/shard_map/while
  806.6 1.0 copy-start.16
  807.6 0.7 copy-start.1
